TPU v7x, 32 devices: a whole 2x2x4 slice. The times are simulated.
32 devices in a mesh: section: 4 (over y, x), dp: 8 (over z, core).
Axes of the slice: x: 2, y: 2, z: 4, core: 2. Of those that a mesh axis runs over, the one named last changes fastest.
Arguments:
- tokens: bfloat16 [2, 4, 448, 2048], P(None, None, 'dp'), may hold values from -6 to 6
- targets: bfloat16 [2, 4, 448, 2048], P(None, None, 'dp'), may hold values from -6 to 6
- weights: bfloat16 [4, 2, 2, 96, 128, 128], P('section'), as said below
- pattern: int32 [4, 2, 2, 96, 2], P('section'), may hold values from 0 to 63, as said below
- master: float32 [4, 2, 96, 128, 128], P('section', None, None, 'dp'), may hold values from -0.6 to 0.6
- moment: float32 [4, 2, 96, 128, 128], P('section', None, None, 'dp'), as said below
- variance: float32 [4, 2, 96, 128, 128], P('section', None, None, 'dp'), as said below
Outputs:
- adam_step: float32 [4, 2, 96, 128, 128], P('section', None, None, 'dp')
- new_master: float32 [4, 2, 96, 128, 128], P('section', None, None, 'dp')
Inputs may be any that keep to these rules, and one draw needn't show every extreme that they name: Within one layer and projection the 96 blocks are distinct and sorted; every block column of the up projection and every block row of the down projection holds one or more blocks. pattern[s,1] equals pattern[3 - s, 0]. Up blocks have rows below 16 and columns below 64, down blocks the reverse. weights[s,1] equals weights[3 - s, 0]; entries are scaled by the inverse root of the mean number of inputs per output. `moment`: of the order of the gradient. `variance`: Positive, of the order of the squared gradient.
All inputs are finite; a program needn't handle non-finite values.
Results may differ from a plain program's by a relative error of at most 0.022.
Values may be sent and summed in bfloat16 or wider, within the bound.
No kernel may reach another device: no remote copies, remote signals or barrier semaphores. Data moves between devices by JAX's collectives and lax.ppermute only.
A program may use at most 192 MiB of HBM per device.

v0:
```python
import jax
import jax.numpy as jnp
from jax import lax
from jax.sharding import PartitionSpec as P

D = 2048
FF = 8192
BS = 128


norm_eps = 1e-06
gelu_coef = 0.7978845608028654
beta_first = 0.9
beta_second = 0.95
adam_eps = 1e-08
learn_rate = 0.001
decay_rate = 0.1
update_count = 10


def from_behind(x, axis, by):
    devices = lax.axis_size(axis)
    pairs = [(i, i + by) for i in range(devices) if 0 <= i + by < devices]
    return lax.ppermute(x, axis, pairs)


def partner(x, axis, stride):
    return lax.ppermute(x, axis, [(i, i ^ 1 << stride) for i in range(lax.axis_size(axis))])


def sparse_product(left_rows, blocks, take_index, put_index, out_blocks):
    row_count = left_rows.shape[0]
    picked = jnp.take(left_rows.reshape(row_count, -1, BS), take_index, axis=1)
    product = jnp.einsum("rka,kab->krb", picked, blocks, preferred_element_type=jnp.float32)
    summed = jax.ops.segment_sum(product, put_index, num_segments=out_blocks)
    return summed.transpose(1, 0, 2).reshape(row_count, out_blocks * BS)


def sparse_transposed(left_rows, blocks, take_index, put_index, out_blocks):
    row_count = left_rows.shape[0]
    picked = jnp.take(left_rows.reshape(row_count, -1, BS), take_index, axis=1)
    product = jnp.einsum("rkb,kab->kra", picked, blocks, preferred_element_type=jnp.float32)
    summed = jax.ops.segment_sum(product, put_index, num_segments=out_blocks)
    return summed.transpose(1, 0, 2).reshape(row_count, out_blocks * BS)


def gelu_slope(preact):
    tanh_input = gelu_coef * (preact + 0.044715 * preact**3)
    tangent = jnp.tanh(tanh_input)
    return 0.5 * (1.0 + tangent) + 0.5 * preact * (1.0 - tangent * tangent) * gelu_coef * (
        1.0 + 3.0 * 0.044715 * preact * preact
    )


def layer_forward(inputs, layer_weights, layer_pattern):
    widened = inputs.astype(jnp.float32)
    factor = lax.rsqrt(jnp.mean(widened * widened, axis=-1, keepdims=True) + norm_eps)
    normed = (widened * factor).astype(jnp.bfloat16)
    preact = sparse_product(
        normed, layer_weights[0], layer_pattern[0, :, 0], layer_pattern[0, :, 1], FF // BS
    )
    hidden = jax.nn.gelu(preact, approximate=True).astype(jnp.bfloat16)
    mixed = sparse_product(
        hidden, layer_weights[1], layer_pattern[1, :, 0], layer_pattern[1, :, 1], D // BS
    )
    result = (widened + mixed).astype(jnp.bfloat16)
    return (result, normed, preact, hidden)


def layer_backward(inputs, preact, upstream, layer_weights, layer_pattern):
    grad_hidden = sparse_transposed(
        upstream, layer_weights[1], layer_pattern[1, :, 1], layer_pattern[1, :, 0], FF // BS
    )
    grad_preact = (grad_hidden * gelu_slope(preact)).astype(jnp.bfloat16)
    grad_normed = sparse_transposed(
        grad_preact, layer_weights[0], layer_pattern[0, :, 1], layer_pattern[0, :, 0], D // BS
    )
    widened = inputs.astype(jnp.float32)
    factor = lax.rsqrt(jnp.mean(widened * widened, axis=-1, keepdims=True) + norm_eps)
    coupling = jnp.mean(widened * grad_normed, axis=-1, keepdims=True)
    downstream = (
        upstream.astype(jnp.float32) + factor * grad_normed - widened * factor**3 * coupling
    )
    return (downstream.astype(jnp.bfloat16), grad_preact)


def block_pairs(left_rows, right_rows, left_index, right_index):
    row_count = left_rows.shape[0]
    left_picked = jnp.take(left_rows.reshape(row_count, -1, BS), left_index, axis=1)
    right_picked = jnp.take(right_rows.reshape(row_count, -1, BS), right_index, axis=1)
    return jnp.einsum("rka,rkb->kab", left_picked, right_picked, preferred_element_type=jnp.float32)


def weight_grads(normed, grad_preact, hidden, upstream, layer_pattern):
    up_part = block_pairs(normed, grad_preact, layer_pattern[0, :, 0], layer_pattern[0, :, 1])
    down_part = block_pairs(hidden, upstream, layer_pattern[1, :, 0], layer_pattern[1, :, 1])
    return jnp.stack([up_part, down_part])


def adam_update(grad_sum, master, moment, variance, token_total):
    gradient = grad_sum / token_total
    moment_next = beta_first * moment + (1.0 - beta_first) * gradient
    variance_next = beta_second * variance + (1.0 - beta_second) * gradient * gradient
    corrected = moment_next / (1.0 - beta_first**update_count)
    spread = jnp.sqrt(variance_next / (1.0 - beta_second**update_count))
    step_direction = corrected / (spread + adam_eps)
    return (step_direction, master - learn_rate * (step_direction + decay_rate * master))


def keep_slot(store, stream, slot_index, active, value):
    previous = store[stream, slot_index]
    return store.at[stream, slot_index].set(jnp.where(active, value, previous))


def shards(tokens, targets, weights, pattern, master, moment, variance):
    section_index = lax.axis_index("section")
    section_count = lax.axis_size("section")
    micro_count = tokens.shape[1]
    row_count = tokens.shape[2]
    tick_count = section_count + micro_count - 1
    local_weights = weights[0]
    local_pattern = pattern[0]
    forward_place = (section_index, section_count - 1 - section_index)
    backward_place = (section_count - 1 - section_index, section_index)

    def stream_forward(stream, tick_index, received, stores):
        slot_raw = tick_index - forward_place[stream]
        active = (slot_raw >= 0) & (slot_raw < micro_count)
        slot_index = jnp.clip(slot_raw, 0, micro_count - 1)
        entering = lax.dynamic_index_in_dim(tokens[stream], slot_index, 0, keepdims=False)
        inputs = jnp.where(forward_place[stream] == 0, entering, received)

        def live_branch(values):
            return layer_forward(values, local_weights[stream], local_pattern[stream])

        def dead_branch(values):
            return (
                jnp.zeros((row_count, D), jnp.bfloat16),
                jnp.zeros((row_count, D), jnp.bfloat16),
                jnp.zeros((row_count, FF), jnp.float32),
                jnp.zeros((row_count, FF), jnp.bfloat16),
            )

        result, normed, preact, hidden = lax.cond(active, live_branch, dead_branch, inputs)
        target_rows = lax.dynamic_index_in_dim(targets[stream], slot_index, 0, keepdims=False)
        residue = (result.astype(jnp.float32) - target_rows.astype(jnp.float32)).astype(
            jnp.bfloat16
        )
        fresh_values = (inputs, normed, preact, hidden, residue)
        stores = tuple(
            (
                keep_slot(store, stream, slot_index, active, value)
                for store, value in zip(stores, fresh_values)
            )
        )
        return (result, stores)

    def forward_tick(state_now, tick_index):
        received_down, received_up, stores = state_now
        result_down, stores = stream_forward(0, tick_index, received_down, stores)
        result_up, stores = stream_forward(1, tick_index, received_up, stores)
        received_down = from_behind(result_down, "section", 1)
        received_up = from_behind(result_up, "section", -1)
        return ((received_down, received_up, stores), None)

    empty_rows = jnp.zeros((row_count, D), jnp.bfloat16)
    forward_stores = (
        jnp.zeros((2, micro_count, row_count, D), jnp.bfloat16),
        jnp.zeros((2, micro_count, row_count, D), jnp.bfloat16),
        jnp.zeros((2, micro_count, row_count, FF), jnp.float32),
        jnp.zeros((2, micro_count, row_count, FF), jnp.bfloat16),
        jnp.zeros((2, micro_count, row_count, D), jnp.bfloat16),
    )
    forward_state, unused = lax.scan(
        forward_tick, (empty_rows, empty_rows, forward_stores), jnp.arange(tick_count)
    )
    saved_inputs, saved_normed, saved_preact, saved_hidden, saved_residue = forward_state[2]

    def stream_backward(stream, tick_index, received, stores):
        slot_raw = tick_index - backward_place[stream]
        active = (slot_raw >= 0) & (slot_raw < micro_count)
        slot_index = jnp.clip(slot_raw, 0, micro_count - 1)
        upstream = jnp.where(
            backward_place[stream] == 0, saved_residue[stream, slot_index], received
        )

        def live_branch(operands):
            return layer_backward(
                operands[0], operands[1], operands[2], local_weights[stream], local_pattern[stream]
            )

        def dead_branch(operands):
            return (
                jnp.zeros((row_count, D), jnp.bfloat16),
                jnp.zeros((row_count, FF), jnp.bfloat16),
            )

        operands = (saved_inputs[stream, slot_index], saved_preact[stream, slot_index], upstream)
        downstream, grad_preact = lax.cond(active, live_branch, dead_branch, operands)
        stores = (
            keep_slot(stores[0], stream, slot_index, active, grad_preact),
            keep_slot(stores[1], stream, slot_index, active, upstream),
        )
        return (downstream, stores)

    def backward_tick(state_now, tick_index):
        received_down, received_up, stores = state_now
        result_down, stores = stream_backward(0, tick_index, received_down, stores)
        result_up, stores = stream_backward(1, tick_index, received_up, stores)
        received_down = from_behind(result_down, "section", -1)
        received_up = from_behind(result_up, "section", 1)
        return ((received_down, received_up, stores), None)

    backward_stores = (
        jnp.zeros((2, micro_count, row_count, FF), jnp.bfloat16),
        jnp.zeros((2, micro_count, row_count, D), jnp.bfloat16),
    )
    backward_state, unused = lax.scan(
        backward_tick, (empty_rows, empty_rows, backward_stores), jnp.arange(tick_count)
    )
    saved_grad_preact, saved_upstream = backward_state[2]

    def copy_grads(stream):
        return weight_grads(
            saved_normed[stream].reshape(-1, D),
            saved_grad_preact[stream].reshape(-1, FF),
            saved_hidden[stream].reshape(-1, FF),
            saved_upstream[stream].reshape(-1, D),
            local_pattern[stream],
        )

    own_share = lax.psum_scatter(
        copy_grads(0).astype(jnp.bfloat16), "dp", scatter_dimension=2, tiled=True
    ).astype(jnp.float32)
    other_share = lax.psum_scatter(
        copy_grads(1).astype(jnp.bfloat16), "dp", scatter_dimension=2, tiled=True
    ).astype(jnp.float32)
    bit_total = section_count.bit_length() - 1
    bit_order = list(range(bit_total))
    arrived = other_share
    for bit_number in bit_order:
        arrived = partner(arrived.astype(jnp.bfloat16), "section", bit_number).astype(arrived.dtype)
    token_total = 2 * micro_count * row_count * lax.axis_size("dp")
    step_direction, master_next = adam_update(
        own_share + arrived, master[0], moment[0], variance[0], token_total
    )
    return (step_direction[None], master_next[None])


def solution(mesh):
    return jax.shard_map(
        shards,
        mesh=mesh,
        in_specs=(
            P(None, None, "dp", None),
            P(None, None, "dp", None),
            P("section", None, None, None, None, None),
            P("section", None, None, None, None),
            P("section", None, None, "dp", None),
            P("section", None, None, "dp", None),
            P("section", None, None, "dp", None),
        ),
        out_specs=(P("section", None, None, "dp", None), P("section", None, None, "dp", None)),
        check_vma=False,
    )
```

profile of v0, /device:TPU:0, one launch (start us, length us, event | category | flops | bytes accessed | tf_op | source)
XLA Modules:
  0.0 1634.0 jit_solution(4916698706675204082)
XLA Ops:
  25.2 686.1 %while.54 = (s32[]{:T(128)}, bf16[56,2048]{1,0:T(8,128)(2,1)}, bf16[56,2048]{1,0:T(8,128)(2,1)}, bf16[2,4,56,2048]{3,2,1,0:T(8,128)(2,1)}, bf16[2,4,56,2048]{3,2...) while((s32[]{:T(128)}, bf16[56,2048]{1,0:T(8,128)(2,1)}, ...), condition=%wide.region_13.16_spmd, body=%wide.region_0.15_spmd.sunk | while | flops 735615424 | bytes 153925840 | solution.py:174
  40.7 36.0 %conditional.8 = (bf16[56,2048]{1,0:T(8,128)(2,1)}, bf16[56,2048]{1,0:T(8,128)(2,1)S(1)}, f32[56,8192]{1,0:T(8,128)}, bf16[56,8192]{1,0:T(8,128)(2,1)}, f32[56,2048]{1,0:T(8,128)S(1)}) conditional(s32[]{:T(128)} %convert_element_type.274, () %tuple.240, (bf16[56,2048]{1,0:T(8,128)(2,1)S(1)}, s32[2,2,96,2]{2,3,1,0:T(2,128)S(1)}, ...), branch_computations={%region_1.1_spmd, %region_2.7_spmd} | conditional | flops 364825792 | bytes 48744208 | solution.py:144
  63.9 10.0 scatter_fusion.5
  121.3 36.0 %conditional.8 = (bf16[56,2048]{1,0:T(8,128)(2,1)}, bf16[56,2048]{1,0:T(8,128)(2,1)S(1)}, f32[56,8192]{1,0:T(8,128)}, bf16[56,8192]{1,0:T(8,128)(2,1)}, f32[56,2048]{1,0:T(8,128)S(1)}) conditional(s32[]{:T(128)} %convert_element_type.274, () %tuple.240, (bf16[56,2048]{1,0:T(8,128)(2,1)S(1)}, s32[2,2,96,2]{2,3,1,0:T(2,128)S(1)}, ...), branch_computations={%region_1.1_spmd, %region_2.7_spmd} | conditional | flops 364825792 | bytes 48744208 | solution.py:144
  205.1 36.0 %conditional.8 = (bf16[56,2048]{1,0:T(8,128)(2,1)}, bf16[56,2048]{1,0:T(8,128)(2,1)S(1)}, f32[56,8192]{1,0:T(8,128)}, bf16[56,8192]{1,0:T(8,128)(2,1)}, f32[56,2048]{1,0:T(8,128)S(1)}) conditional(s32[]{:T(128)} %convert_element_type.274, () %tuple.240, (bf16[56,2048]{1,0:T(8,128)(2,1)S(1)}, s32[2,2,96,2]{2,3,1,0:T(2,128)S(1)}, ...), branch_computations={%region_1.1_spmd, %region_2.7_spmd} | conditional | flops 364825792 | bytes 48744208 | solution.py:144
  241.1 34.9 %collective-permute-start = (bf16[56,2048]{1,0:T(8,128)(2,1)}, bf16[56,2048]{1,0:T(8,128)(2,1)}, u32[]{:S(2)}, u32[]{:S(2)}) collective-permute-start(bf16[56,2048]{1,0:T(8,128)(2,1)} %get-tuple-element.991), channel_id=1, source_target_pairs={{0,8},{8,16},{16,24},{1,9},{9,17},{17,25},{2,10},{10,18},{18,26},{... | collective-permute-start | bytes 688136 | tf_op jit(solution)/shard_map/while/body/eval_jaxpr/ppermute | solution.py:24
  313.4 36.2 %conditional.9 = (bf16[56,2048]{1,0:T(8,128)(2,1)}, bf16[56,2048]{1,0:T(8,128)(2,1)S(1)}, f32[56,8192]{1,0:T(8,128)}, bf16[56,8192]{1,0:T(8,128)(2,1)}, f32[56,2048]{1,0:T(8,128)}) conditional(s32[]{:T(128)} %convert_element_type.275, () %tuple.242, (bf16[56,2048]{1,0:T(8,128)(2,1)S(1)}, s32[2,2,96,2]{2,3,1,0:T(2,128)S(1)}, ...), branch_computations={%region_6.8_spmd, %region_7.12_spmd} | conditional | flops 364825792 | bytes 48744208 | solution.py:144
  336.5 10.0 scatter_fusion.7
  350.9 36.0 %conditional.8 = (bf16[56,2048]{1,0:T(8,128)(2,1)}, bf16[56,2048]{1,0:T(8,128)(2,1)S(1)}, f32[56,8192]{1,0:T(8,128)}, bf16[56,8192]{1,0:T(8,128)(2,1)}, f32[56,2048]{1,0:T(8,128)S(1)}) conditional(s32[]{:T(128)} %convert_element_type.274, () %tuple.240, (bf16[56,2048]{1,0:T(8,128)(2,1)S(1)}, s32[2,2,96,2]{2,3,1,0:T(2,128)S(1)}, ...), branch_computations={%region_1.1_spmd, %region_2.7_spmd} | conditional | flops 364825792 | bytes 48744208 | solution.py:144
  435.1 36.2 %conditional.9 = (bf16[56,2048]{1,0:T(8,128)(2,1)}, bf16[56,2048]{1,0:T(8,128)(2,1)S(1)}, f32[56,8192]{1,0:T(8,128)}, bf16[56,8192]{1,0:T(8,128)(2,1)}, f32[56,2048]{1,0:T(8,128)}) conditional(s32[]{:T(128)} %convert_element_type.275, () %tuple.242, (bf16[56,2048]{1,0:T(8,128)(2,1)S(1)}, s32[2,2,96,2]{2,3,1,0:T(2,128)S(1)}, ...), branch_computations={%region_6.8_spmd, %region_7.12_spmd} | conditional | flops 364825792 | bytes 48744208 | solution.py:144
  458.2 10.0 scatter_fusion.7
  475.7 38.4 %collective-permute-start = (bf16[56,2048]{1,0:T(8,128)(2,1)}, bf16[56,2048]{1,0:T(8,128)(2,1)}, u32[]{:S(2)}, u32[]{:S(2)}) collective-permute-start(bf16[56,2048]{1,0:T(8,128)(2,1)} %get-tuple-element.991), channel_id=1, source_target_pairs={{0,8},{8,16},{16,24},{1,9},{9,17},{17,25},{2,10},{10,18},{18,26},{... | collective-permute-start | bytes 688136 | tf_op jit(solution)/shard_map/while/body/eval_jaxpr/ppermute | solution.py:24
  551.3 36.2 %conditional.9 = (bf16[56,2048]{1,0:T(8,128)(2,1)}, bf16[56,2048]{1,0:T(8,128)(2,1)S(1)}, f32[56,8192]{1,0:T(8,128)}, bf16[56,8192]{1,0:T(8,128)(2,1)}, f32[56,2048]{1,0:T(8,128)}) conditional(s32[]{:T(128)} %convert_element_type.275, () %tuple.242, (bf16[56,2048]{1,0:T(8,128)(2,1)S(1)}, s32[2,2,96,2]{2,3,1,0:T(2,128)S(1)}, ...), branch_computations={%region_6.8_spmd, %region_7.12_spmd} | conditional | flops 364825792 | bytes 48744208 | solution.py:144
  574.5 10.0 scatter_fusion.7
  637.6 36.2 %conditional.9 = (bf16[56,2048]{1,0:T(8,128)(2,1)}, bf16[56,2048]{1,0:T(8,128)(2,1)S(1)}, f32[56,8192]{1,0:T(8,128)}, bf16[56,8192]{1,0:T(8,128)(2,1)}, f32[56,2048]{1,0:T(8,128)}) conditional(s32[]{:T(128)} %convert_element_type.275, () %tuple.242, (bf16[56,2048]{1,0:T(8,128)(2,1)S(1)}, s32[2,2,96,2]{2,3,1,0:T(2,128)S(1)}, ...), branch_computations={%region_6.8_spmd, %region_7.12_spmd} | conditional | flops 364825792 | bytes 48744208 | solution.py:144
  660.7 10.0 scatter_fusion.7
  716.1 702.9 %while.55 = (s32[]{:T(128)}, bf16[56,2048]{1,0:T(8,128)(2,1)S(1)}, bf16[56,2048]{1,0:T(8,128)(2,1)}, bf16[2,4,56,8192]{3,2,1,0:T(8,128)(2,1)}, bf16[2,4,56,2048]...) while((s32[]{:T(128)}, bf16[56,2048]{1,0:T(8,128)(2,1)S(1)}, ...), condition=%wide.region_29.33_spmd, body=%wide.region_14.32_spmd.sunk | while | flops 750754432 | bytes 148414816 | solution.py:218
  736.5 46.6 %conditional.11 = (bf16[56,2048]{1,0:T(8,128)(2,1)}, bf16[56,8192]{1,0:T(8,128)(2,1)}) conditional(s32[]{:T(128)} %convert_element_type.277, () %tuple.250, (bf16[56,2048]{1,0:T(8,128)(2,1)S(1)}, bf16[2,4,56,2048]{3,2,1,0:T(8,128)(2,1)}, s32[]{:T(128)}, s32[2,2,96,2]{2,3,1,0:T(2,128)S(1)}, bf16[2,2,96,128,128]{4,3,2,1,0:T(8,128)(2,1)}, ...), branch_computations={%region_21.24_spmd, %region_22.29_spmd} | conditional | flops 374115616 | bytes 59755372 | solution.py:199
  743.3 10.0 scatter_fusion.2
  765.1 10.0 scatter_fusion.3
  802.2 46.6 %conditional.11 = (bf16[56,2048]{1,0:T(8,128)(2,1)}, bf16[56,8192]{1,0:T(8,128)(2,1)}) conditional(s32[]{:T(128)} %convert_element_type.277, () %tuple.250, (bf16[56,2048]{1,0:T(8,128)(2,1)S(1)}, bf16[2,4,56,2048]{3,2,1,0:T(8,128)(2,1)}, s32[]{:T(128)}, s32[2,2,96,2]{2,3,1,0:T(2,128)S(1)}, bf16[2,2,96,128,128]{4,3,2,1,0:T(8,128)(2,1)}, ...), branch_computations={%region_21.24_spmd, %region_22.29_spmd} | conditional | flops 374115616 | bytes 59755372 | solution.py:199
  809.0 10.0 scatter_fusion.2
  830.8 10.0 scatter_fusion.3
  870.0 46.6 %conditional.11 = (bf16[56,2048]{1,0:T(8,128)(2,1)}, bf16[56,8192]{1,0:T(8,128)(2,1)}) conditional(s32[]{:T(128)} %convert_element_type.277, () %tuple.250, (bf16[56,2048]{1,0:T(8,128)(2,1)S(1)}, bf16[2,4,56,2048]{3,2,1,0:T(8,128)(2,1)}, s32[]{:T(128)}, s32[2,2,96,2]{2,3,1,0:T(2,128)S(1)}, bf16[2,2,96,128,128]{4,3,2,1,0:T(8,128)(2,1)}, ...), branch_computations={%region_21.24_spmd, %region_22.29_spmd} | conditional | flops 374115616 | bytes 59755372 | solution.py:199
  876.9 10.0 scatter_fusion.2
  898.7 10.0 scatter_fusion.3
  916.6 31.4 %collective-permute-start.3 = (bf16[56,2048]{1,0:T(8,128)(2,1)}, bf16[56,2048]{1,0:T(8,128)(2,1)}, u32[]{:S(2)}, u32[]{:S(2)}) collective-permute-start(bf16[56,2048]{1,0:T(8,128)(2,1)} %get-tuple-element.1031), channel_id=1, source_target_pairs={{0,8},{8,16},{16,24},{1,9},{9,17},{17,25},{2,10},{10,18},{18,26},{... | collective-permute-start | bytes 688136 | tf_op jit(solution)/shard_map/while/body/eval_jaxpr/ppermute | solution.py:24
  957.8 44.8 %collective-permute-done.2 = bf16[56,2048]{1,0:T(8,128)(2,1)S(1)} collective-permute-done((bf16[56,2048]{1,0:T(8,128)(2,1)S(1)}, bf16[56,2048]{1,0:T(8,128)(2,1)S(1)}, u32[]{:S(2)}, u32[]{:S(2)}) %collective-permute-start.2) | collective-permute-done | bytes 229408 | tf_op jit(solution)/shard_map/while/body/eval_jaxpr/ppermute | solution.py:24
  1010.0 46.6 %conditional.11 = (bf16[56,2048]{1,0:T(8,128)(2,1)}, bf16[56,8192]{1,0:T(8,128)(2,1)}) conditional(s32[]{:T(128)} %convert_element_type.277, () %tuple.250, (bf16[56,2048]{1,0:T(8,128)(2,1)S(1)}, bf16[2,4,56,2048]{3,2,1,0:T(8,128)(2,1)}, s32[]{:T(128)}, s32[2,2,96,2]{2,3,1,0:T(2,128)S(1)}, bf16[2,2,96,128,128]{4,3,2,1,0:T(8,128)(2,1)}, ...), branch_computations={%region_21.24_spmd, %region_22.29_spmd} | conditional | flops 374115616 | bytes 59755372 | solution.py:199
  1016.8 10.0 scatter_fusion.2
  1038.6 10.0 scatter_fusion.3
  1063.9 45.9 %conditional.10 = (bf16[56,2048]{1,0:T(8,128)(2,1)S(1)}, bf16[56,8192]{1,0:T(8,128)(2,1)}) conditional(s32[]{:T(128)} %convert_element_type.276, () %tuple.248, (bf16[56,2048]{1,0:T(8,128)(2,1)S(1)}, bf16[2,4,56,2048]{3,2,1,0:T(8,128)(2,1)}, s32[]{:T(128)}, s32[2,2,96,2]{2,3,1,0:T(2,128)S(1)}, bf16[2,2,96,128,128]{4,3,2,1,0:T(8,128)(2,1)}, ...), branch_computations={%region_15.18_spmd, %region_16.23_spmd} | conditional | flops 374115616 | bytes 59755372 | solution.py:199
  1070.8 10.0 scatter_fusion
  1092.6 10.0 scatter_fusion.1
  1128.8 50.4 %collective-permute-start.3 = (bf16[56,2048]{1,0:T(8,128)(2,1)}, bf16[56,2048]{1,0:T(8,128)(2,1)}, u32[]{:S(2)}, u32[]{:S(2)}) collective-permute-start(bf16[56,2048]{1,0:T(8,128)(2,1)} %get-tuple-element.1031), channel_id=1, source_target_pairs={{0,8},{8,16},{16,24},{1,9},{9,17},{17,25},{2,10},{10,18},{18,26},{... | collective-permute-start | bytes 688136 | tf_op jit(solution)/shard_map/while/body/eval_jaxpr/ppermute | solution.py:24
  1179.2 45.9 %conditional.10 = (bf16[56,2048]{1,0:T(8,128)(2,1)S(1)}, bf16[56,8192]{1,0:T(8,128)(2,1)}) conditional(s32[]{:T(128)} %convert_element_type.276, () %tuple.248, (bf16[56,2048]{1,0:T(8,128)(2,1)S(1)}, bf16[2,4,56,2048]{3,2,1,0:T(8,128)(2,1)}, s32[]{:T(128)}, s32[2,2,96,2]{2,3,1,0:T(2,128)S(1)}, bf16[2,2,96,128,128]{4,3,2,1,0:T(8,128)(2,1)}, ...), branch_computations={%region_15.18_spmd, %region_16.23_spmd} | conditional | flops 374115616 | bytes 59755372 | solution.py:199
  1186.1 10.0 scatter_fusion
  1207.9 10.0 scatter_fusion.1
  1249.7 45.9 %conditional.10 = (bf16[56,2048]{1,0:T(8,128)(2,1)S(1)}, bf16[56,8192]{1,0:T(8,128)(2,1)}) conditional(s32[]{:T(128)} %convert_element_type.276, () %tuple.248, (bf16[56,2048]{1,0:T(8,128)(2,1)S(1)}, bf16[2,4,56,2048]{3,2,1,0:T(8,128)(2,1)}, s32[]{:T(128)}, s32[2,2,96,2]{2,3,1,0:T(2,128)S(1)}, bf16[2,2,96,128,128]{4,3,2,1,0:T(8,128)(2,1)}, ...), branch_computations={%region_15.18_spmd, %region_16.23_spmd} | conditional | flops 374115616 | bytes 59755372 | solution.py:199
  1256.6 10.0 scatter_fusion
  1278.4 10.0 scatter_fusion.1
  1304.4 44.2 %collective-permute-done.2 = bf16[56,2048]{1,0:T(8,128)(2,1)S(1)} collective-permute-done((bf16[56,2048]{1,0:T(8,128)(2,1)S(1)}, bf16[56,2048]{1,0:T(8,128)(2,1)S(1)}, u32[]{:S(2)}, u32[]{:S(2)}) %collective-permute-start.2) | collective-permute-done | bytes 229408 | tf_op jit(solution)/shard_map/while/body/eval_jaxpr/ppermute | solution.py:24
  1363.9 45.9 %conditional.10 = (bf16[56,2048]{1,0:T(8,128)(2,1)S(1)}, bf16[56,8192]{1,0:T(8,128)(2,1)}) conditional(s32[]{:T(128)} %convert_element_type.276, () %tuple.248, (bf16[56,2048]{1,0:T(8,128)(2,1)S(1)}, bf16[2,4,56,2048]{3,2,1,0:T(8,128)(2,1)}, s32[]{:T(128)}, s32[2,2,96,2]{2,3,1,0:T(2,128)S(1)}, bf16[2,2,96,128,128]{4,3,2,1,0:T(8,128)(2,1)}, ...), branch_computations={%region_15.18_spmd, %region_16.23_spmd} | conditional | flops 374115616 | bytes 59755372 | solution.py:199
  1370.7 10.0 scatter_fusion
  1392.6 10.0 scatter_fusion.1
  1532.2 19.1 %reduce-scatter.5.cloned.1.call-done = bf16[2,96,16,128]{3,2,1,0:T(8,128)(2,1)} async-done(((bf16[2,96,128,128]{3,2,1,0:T(8,128)(2,1)}), bf16[2,96,16,128]{3,2,1,0:T(8,128)(2,1)}) %reduce-scatter.5.cloned.1.call-update) | async-done | bytes 786448 | tf_op jit(solution)/shard_map/reduce_scatter | solution.py:235
  1552.8 16.3 collective-permute-done.4
  1570.5 51.3 %reduce-scatter.3.cloned.1.call-done = bf16[2,96,16,128]{3,2,1,0:T(8,128)(2,1)} async-done(((bf16[2,96,128,128]{3,2,1,0:T(8,128)(2,1)}), bf16[2,96,16,128]{3,2,1,0:T(8,128)(2,1)}) %reduce-scatter.3.cloned.1.call-update) | async-done | bytes 786448 | tf_op jit(solution)/shard_map/reduce_scatter | solution.py:232
  (858 shorter events, 1073.0 us)
Async XLA Ops:
  7.2 1544.1 %reduce-scatter.5.cloned.1.call-start = ((), (), s32[]{:S(2)}) async-start(), calls=%async_computation.3 | async-start | bytes 7077888 | tf_op jit(solution)/shard_map/reduce_scatter | solution.py:235
  39.4 66.4 %collective-permute-start.1 = (bf16[56,2048]{1,0:T(8,128)(2,1)}, bf16[56,2048]{1,0:T(8,128)(2,1)}, u32[]{:S(2)}, u32[]{:S(2)}) collective-permute-start(bf16[56,2048]{1,0:T(8,128)(2,1)} %get-tuple-element.996), channel_id=1, source_target_pairs={{8,0},{16,8},{24,16},{9,1},{17,9},{25,17},{10,2},{18,10},{26,18},{... | collective-permute-start | bytes 688136 | tf_op jit(solution)/shard_map/while/body/eval_jaxpr/ppermute | solution.py:24
  76.8 29.0 %collective-permute-start = (bf16[56,2048]{1,0:T(8,128)(2,1)}, bf16[56,2048]{1,0:T(8,128)(2,1)}, u32[]{:S(2)}, u32[]{:S(2)}) collective-permute-start(bf16[56,2048]{1,0:T(8,128)(2,1)} %get-tuple-element.991), channel_id=1, source_target_pairs={{0,8},{8,16},{16,24},{1,9},{9,17},{17,25},{2,10},{10,18},{18,26},{... | collective-permute-start | bytes 688136 | tf_op jit(solution)/shard_map/while/body/eval_jaxpr/ppermute | solution.py:24
  120.0 69.6 %collective-permute-start.1 = (bf16[56,2048]{1,0:T(8,128)(2,1)}, bf16[56,2048]{1,0:T(8,128)(2,1)}, u32[]{:S(2)}, u32[]{:S(2)}) collective-permute-start(bf16[56,2048]{1,0:T(8,128)(2,1)} %get-tuple-element.996), channel_id=1, source_target_pairs={{8,0},{16,8},{24,16},{9,1},{17,9},{25,17},{10,2},{18,10},{26,18},{... | collective-permute-start | bytes 688136 | tf_op jit(solution)/shard_map/while/body/eval_jaxpr/ppermute | solution.py:24
  157.3 7.2 copy-start.4
  157.3 32.2 %collective-permute-start = (bf16[56,2048]{1,0:T(8,128)(2,1)}, bf16[56,2048]{1,0:T(8,128)(2,1)}, u32[]{:S(2)}, u32[]{:S(2)}) collective-permute-start(bf16[56,2048]{1,0:T(8,128)(2,1)} %get-tuple-element.991), channel_id=1, source_target_pairs={{0,8},{8,16},{16,24},{1,9},{9,17},{17,25},{2,10},{10,18},{18,26},{... | collective-permute-start | bytes 688136 | tf_op jit(solution)/shard_map/while/body/eval_jaxpr/ppermute | solution.py:24
  203.8 99.3 %collective-permute-start.1 = (bf16[56,2048]{1,0:T(8,128)(2,1)}, bf16[56,2048]{1,0:T(8,128)(2,1)}, u32[]{:S(2)}, u32[]{:S(2)}) collective-permute-start(bf16[56,2048]{1,0:T(8,128)(2,1)} %get-tuple-element.996), channel_id=1, source_target_pairs={{8,0},{16,8},{24,16},{9,1},{17,9},{25,17},{10,2},{18,10},{26,18},{... | collective-permute-start | bytes 688136 | tf_op jit(solution)/shard_map/while/body/eval_jaxpr/ppermute | solution.py:24
  241.1 36.9 %copy-start.4 = (bf16[56,2048]{1,0:T(8,128)(2,1)}, bf16[56,2048]{1,0:T(8,128)(2,1)S(1)}, u32[]{:S(2)}) copy-start(bf16[56,2048]{1,0:T(8,128)(2,1)S(1)} %get-tuple-element.1000) | copy-start | bytes 688132 | tf_op jit(solution)/shard_map/while
  241.1 62.0 %collective-permute-start = (bf16[56,2048]{1,0:T(8,128)(2,1)}, bf16[56,2048]{1,0:T(8,128)(2,1)}, u32[]{:S(2)}, u32[]{:S(2)}) collective-permute-start(bf16[56,2048]{1,0:T(8,128)(2,1)} %get-tuple-element.991), channel_id=1, source_target_pairs={{0,8},{8,16},{16,24},{1,9},{9,17},{17,25},{2,10},{10,18},{18,26},{... | collective-permute-start | bytes 688136 | tf_op jit(solution)/shard_map/while/body/eval_jaxpr/ppermute | solution.py:24
  349.6 75.3 %collective-permute-start.1 = (bf16[56,2048]{1,0:T(8,128)(2,1)}, bf16[56,2048]{1,0:T(8,128)(2,1)}, u32[]{:S(2)}, u32[]{:S(2)}) collective-permute-start(bf16[56,2048]{1,0:T(8,128)(2,1)} %get-tuple-element.996), channel_id=1, source_target_pairs={{8,0},{16,8},{24,16},{9,1},{17,9},{25,17},{10,2},{18,10},{26,18},{... | collective-permute-start | bytes 688136 | tf_op jit(solution)/shard_map/while/body/eval_jaxpr/ppermute | solution.py:24
  386.9 10.1 copy-start.4
  386.9 37.9 %collective-permute-start = (bf16[56,2048]{1,0:T(8,128)(2,1)}, bf16[56,2048]{1,0:T(8,128)(2,1)}, u32[]{:S(2)}, u32[]{:S(2)}) collective-permute-start(bf16[56,2048]{1,0:T(8,128)(2,1)} %get-tuple-element.991), channel_id=1, source_target_pairs={{0,8},{8,16},{16,24},{1,9},{9,17},{17,25},{2,10},{10,18},{18,26},{... | collective-permute-start | bytes 688136 | tf_op jit(solution)/shard_map/while/body/eval_jaxpr/ppermute | solution.py:24
  471.3 69.7 %collective-permute-start.1 = (bf16[56,2048]{1,0:T(8,128)(2,1)}, bf16[56,2048]{1,0:T(8,128)(2,1)}, u32[]{:S(2)}, u32[]{:S(2)}) collective-permute-start(bf16[56,2048]{1,0:T(8,128)(2,1)} %get-tuple-element.996), channel_id=1, source_target_pairs={{8,0},{16,8},{24,16},{9,1},{17,9},{25,17},{10,2},{18,10},{26,18},{... | collective-permute-start | bytes 688136 | tf_op jit(solution)/shard_map/while/body/eval_jaxpr/ppermute | solution.py:24
  475.7 40.3 %copy-start.4 = (bf16[56,2048]{1,0:T(8,128)(2,1)}, bf16[56,2048]{1,0:T(8,128)(2,1)S(1)}, u32[]{:S(2)}) copy-start(bf16[56,2048]{1,0:T(8,128)(2,1)S(1)} %get-tuple-element.1000) | copy-start | bytes 688132 | tf_op jit(solution)/shard_map/while
  475.7 65.3 %collective-permute-start = (bf16[56,2048]{1,0:T(8,128)(2,1)}, bf16[56,2048]{1,0:T(8,128)(2,1)}, u32[]{:S(2)}, u32[]{:S(2)}) collective-permute-start(bf16[56,2048]{1,0:T(8,128)(2,1)} %get-tuple-element.991), channel_id=1, source_target_pairs={{0,8},{8,16},{16,24},{1,9},{9,17},{17,25},{2,10},{10,18},{18,26},{... | collective-permute-start | bytes 688136 | tf_op jit(solution)/shard_map/while/body/eval_jaxpr/ppermute | solution.py:24
  587.5 39.8 %collective-permute-start.1 = (bf16[56,2048]{1,0:T(8,128)(2,1)}, bf16[56,2048]{1,0:T(8,128)(2,1)}, u32[]{:S(2)}, u32[]{:S(2)}) collective-permute-start(bf16[56,2048]{1,0:T(8,128)(2,1)} %get-tuple-element.996), channel_id=1, source_target_pairs={{8,0},{16,8},{24,16},{9,1},{17,9},{25,17},{10,2},{18,10},{26,18},{... | collective-permute-start | bytes 688136 | tf_op jit(solution)/shard_map/while/body/eval_jaxpr/ppermute | solution.py:24
  591.9 10.2 copy-start.4
  591.9 35.3 %collective-permute-start = (bf16[56,2048]{1,0:T(8,128)(2,1)}, bf16[56,2048]{1,0:T(8,128)(2,1)}, u32[]{:S(2)}, u32[]{:S(2)}) collective-permute-start(bf16[56,2048]{1,0:T(8,128)(2,1)} %get-tuple-element.991), channel_id=1, source_target_pairs={{0,8},{8,16},{16,24},{1,9},{9,17},{17,25},{2,10},{10,18},{18,26},{... | collective-permute-start | bytes 688136 | tf_op jit(solution)/shard_map/while/body/eval_jaxpr/ppermute | solution.py:24
  673.7 37.6 %collective-permute-start.1 = (bf16[56,2048]{1,0:T(8,128)(2,1)}, bf16[56,2048]{1,0:T(8,128)(2,1)}, u32[]{:S(2)}, u32[]{:S(2)}) collective-permute-start(bf16[56,2048]{1,0:T(8,128)(2,1)} %get-tuple-element.996), channel_id=1, source_target_pairs={{8,0},{16,8},{24,16},{9,1},{17,9},{25,17},{10,2},{18,10},{26,18},{... | collective-permute-start | bytes 688136 | tf_op jit(solution)/shard_map/while/body/eval_jaxpr/ppermute | solution.py:24
  678.1 8.1 copy-start.4
  678.2 33.2 %collective-permute-start = (bf16[56,2048]{1,0:T(8,128)(2,1)}, bf16[56,2048]{1,0:T(8,128)(2,1)}, u32[]{:S(2)}, u32[]{:S(2)}) collective-permute-start(bf16[56,2048]{1,0:T(8,128)(2,1)} %get-tuple-element.991), channel_id=1, source_target_pairs={{0,8},{8,16},{16,24},{1,9},{9,17},{17,25},{2,10},{10,18},{18,26},{... | collective-permute-start | bytes 688136 | tf_op jit(solution)/shard_map/while/body/eval_jaxpr/ppermute | solution.py:24
  783.0 11.8 collective-permute-start.3
  786.0 8.8 collective-permute-start.2
  848.7 14.0 collective-permute-start.3
  853.9 8.8 collective-permute-start.2
  916.6 41.2 %collective-permute-start.3 = (bf16[56,2048]{1,0:T(8,128)(2,1)}, bf16[56,2048]{1,0:T(8,128)(2,1)}, u32[]{:S(2)}, u32[]{:S(2)}) collective-permute-start(bf16[56,2048]{1,0:T(8,128)(2,1)} %get-tuple-element.1031), channel_id=1, source_target_pairs={{0,8},{8,16},{16,24},{1,9},{9,17},{17,25},{2,10},{10,18},{18,26},{... | collective-permute-start | bytes 688136 | tf_op jit(solution)/shard_map/while/body/eval_jaxpr/ppermute | solution.py:24
  949.0 53.6 %collective-permute-start.2 = (bf16[56,2048]{1,0:T(8,128)(2,1)S(1)}, bf16[56,2048]{1,0:T(8,128)(2,1)S(1)}, u32[]{:S(2)}, u32[]{:S(2)}) collective-permute-start(bf16[56,2048]{1,0:T(8,128)(2,1)S(1)} %get-tuple-element.1027), channel_id=1, source_target_pairs={{8,0},{16,8},{24,16},{9,1},{17,9},{25,17},{10,2},{18,10},{26,18},{... | collective-permute-start | bytes 688136 | tf_op jit(solution)/shard_map/while/body/eval_jaxpr/ppermute | solution.py:24
  954.6 48.0 %copy-start.7 = (bf16[2,4,56,2048]{3,2,1,0:T(8,128)(2,1)S(1)}, bf16[2,4,56,2048]{3,2,1,0:T(8,128)(2,1)}, u32[]{:S(2)}) copy-start(bf16[2,4,56,2048]{3,2,1,0:T(8,128)(2,1)} %copy-done.6) | copy-start | bytes 5505028 | tf_op jit(solution)/shard_map/while
  1056.5 63.2 %collective-permute-start.3 = (bf16[56,2048]{1,0:T(8,128)(2,1)}, bf16[56,2048]{1,0:T(8,128)(2,1)}, u32[]{:S(2)}, u32[]{:S(2)}) collective-permute-start(bf16[56,2048]{1,0:T(8,128)(2,1)} %get-tuple-element.1031), channel_id=1, source_target_pairs={{0,8},{8,16},{16,24},{1,9},{9,17},{17,25},{2,10},{10,18},{18,26},{... | collective-permute-start | bytes 688136 | tf_op jit(solution)/shard_map/while/body/eval_jaxpr/ppermute | solution.py:24
  1109.8 10.0 collective-permute-start.2
  1128.8 105.1 %collective-permute-start.3 = (bf16[56,2048]{1,0:T(8,128)(2,1)}, bf16[56,2048]{1,0:T(8,128)(2,1)}, u32[]{:S(2)}, u32[]{:S(2)}) collective-permute-start(bf16[56,2048]{1,0:T(8,128)(2,1)} %get-tuple-element.1031), channel_id=1, source_target_pairs={{0,8},{8,16},{16,24},{1,9},{9,17},{17,25},{2,10},{10,18},{18,26},{... | collective-permute-start | bytes 688136 | tf_op jit(solution)/shard_map/while/body/eval_jaxpr/ppermute | solution.py:24
  1225.1 8.8 collective-permute-start.2
  1242.9 61.4 %collective-permute-start.3 = (bf16[56,2048]{1,0:T(8,128)(2,1)}, bf16[56,2048]{1,0:T(8,128)(2,1)}, u32[]{:S(2)}, u32[]{:S(2)}) collective-permute-start(bf16[56,2048]{1,0:T(8,128)(2,1)} %get-tuple-element.1031), channel_id=1, source_target_pairs={{0,8},{8,16},{16,24},{1,9},{9,17},{17,25},{2,10},{10,18},{18,26},{... | collective-permute-start | bytes 688136 | tf_op jit(solution)/shard_map/while/body/eval_jaxpr/ppermute | solution.py:24
  1295.6 53.0 %collective-permute-start.2 = (bf16[56,2048]{1,0:T(8,128)(2,1)S(1)}, bf16[56,2048]{1,0:T(8,128)(2,1)S(1)}, u32[]{:S(2)}, u32[]{:S(2)}) collective-permute-start(bf16[56,2048]{1,0:T(8,128)(2,1)S(1)} %get-tuple-element.1027), channel_id=1, source_target_pairs={{8,0},{16,8},{24,16},{9,1},{17,9},{25,17},{10,2},{18,10},{26,18},{... | collective-permute-start | bytes 688136 | tf_op jit(solution)/shard_map/while/body/eval_jaxpr/ppermute | solution.py:24
  1302.4 46.2 %copy-start.7 = (bf16[2,4,56,2048]{3,2,1,0:T(8,128)(2,1)S(1)}, bf16[2,4,56,2048]{3,2,1,0:T(8,128)(2,1)}, u32[]{:S(2)}) copy-start(bf16[2,4,56,2048]{3,2,1,0:T(8,128)(2,1)} %copy-done.6) | copy-start | bytes 5505028 | tf_op jit(solution)/shard_map/while
  1357.6 60.9 %collective-permute-start.3 = (bf16[56,2048]{1,0:T(8,128)(2,1)}, bf16[56,2048]{1,0:T(8,128)(2,1)}, u32[]{:S(2)}, u32[]{:S(2)}) collective-permute-start(bf16[56,2048]{1,0:T(8,128)(2,1)} %get-tuple-element.1031), channel_id=1, source_target_pairs={{0,8},{8,16},{16,24},{1,9},{9,17},{17,25},{2,10},{10,18},{18,26},{... | collective-permute-start | bytes 688136 | tf_op jit(solution)/shard_map/while/body/eval_jaxpr/ppermute | solution.py:24
  1409.8 8.8 collective-permute-start.2
  1419.0 7.2 slice-start
  1455.2 12.8 slice-start.4
  1461.2 6.8 slice-start.5
  1479.7 142.2 %reduce-scatter.3.cloned.1.call-start = ((), (), s32[]{:S(2)}) async-start(), calls=%async_computation.2 | async-start | bytes 7077888 | tf_op jit(solution)/shard_map/reduce_scatter | solution.py:232
  1509.4 12.6 slice-start.2
  1513.3 8.7 slice-start.3
  1513.3 8.7 copy-start.10
  1532.2 89.7 %copy-start.12 = (f32[1,2,96,16,128]{4,3,2,1,0:T(8,128)S(1)}, f32[1,2,96,16,128]{4,3,2,1,0:T(8,128)}, u32[]{:S(2)}) copy-start(f32[1,2,96,16,128]{4,3,2,1,0:T(8,128)} %param.59) | copy-start | bytes 4718596
  1532.2 89.7 %copy-start.13 = (f32[1,2,96,16,128]{4,3,2,1,0:T(8,128)S(1)}, f32[1,2,96,16,128]{4,3,2,1,0:T(8,128)}, u32[]{:S(2)}) copy-start(f32[1,2,96,16,128]{4,3,2,1,0:T(8,128)} %param.61) | copy-start | bytes 4718596
  1551.3 17.7 %collective-permute-start.4 = (bf16[2,96,16,128]{3,2,1,0:T(8,128)(2,1)}, bf16[2,96,16,128]{3,2,1,0:T(8,128)(2,1)}, u32[]{:S(2)}, u32[]{:S(2)}) collective-permute-start(bf16[2,96,16,128]{3,2,1,0:T(8,128)(2,1)} %reduce-scatter.5.cloned.1.call-done), channel_id=1, source_target_pairs={{0,8},{8,0},{16,24},{24,16},{1,9},{9,1},{17,25},{25,17},{2,10},{10... | collective-permute-start | bytes 2359304 | tf_op jit(solution)/shard_map/ppermute | solution.py:28
  1569.0 52.8 %collective-permute-start.5 = (bf16[2,96,16,128]{3,2,1,0:T(8,128)(2,1)}, bf16[2,96,16,128]{3,2,1,0:T(8,128)(2,1)}, u32[]{:S(2)}, u32[]{:S(2)}) collective-permute-start(bf16[2,96,16,128]{3,2,1,0:T(8,128)(2,1)} %collective-permute-done.4), channel_id=1, source_target_pairs={{0,16},{8,24},{16,0},{24,8},{1,17},{9,25},{17,1},{25,9},{2,18},{10... | collective-permute-start | bytes 2359304 | tf_op jit(solution)/shard_map/ppermute | solution.py:28
  (50 other events, 160.8 us)
Sparse Core Ops, SparseCore 0:
  1479.8 71.4 reduce-scatter.4
  1553.6 68.1 reduce-scatter.2
where the time goes:
time: 1660 us; the launch traced here: 1630 us
  other arithmetic  655 us (39%)
  local copies, waits for them, and re-layouts  324 us (20%)
  starting transfers between devices  233 us (14%)
  matrix products  196 us (12%)
  waiting for transfers between devices  176 us (11%)
  loops' own time  34.7 us (2%)
    ppermute x28, starting transfers between devices, from_behind(): return lax.ppermute(x, axis, pairs)  230 us
    scatter x91, other arithmetic, keep_slot(): return store.at[stream, slot_index].set(jnp.where(active, value, previous))  205 us
    scatter-add x16, other arithmetic, sparse_transposed(): summed = jax.ops.segment_sum(product, put_index, num_segments=out_blocks)  160 us
    scatter-add x16, other arithmetic, sparse_product(): summed = jax.ops.segment_sum(product, put_index, num_segments=out_blocks)  160 us
    dynamic_slice x98, local copies, waits for them, and re-layouts, keep_slot(): previous = store[stream, slot_index]  97.9 us
    dot_general x16, matrix products, sparse_transposed(): jnp.einsum('rkb,kab->kra', picked, blocks, preferred_element_type=jnp.flo...  95.7 us
    ppermute x28, waiting for transfers between devices, from_behind(): return lax.ppermute(x, axis, pairs)  89.1 us
    dot_general x16, matrix products, sparse_product(): jnp.einsum('rka,kab->krb', picked, blocks, preferred_element_type=jnp.flo...  74.6 us
  transfers between devices with their start and end apart: 32, of which 5 were waited for; matrix products, arithmetic and copies ran while one was open for 39% of the time, Pallas kernels for 0%

commit v1 on v0

v1 whole, which is shorter than its diff:
```python
import functools

import jax
import jax.numpy as jnp
from jax import lax
from jax.experimental import pallas as pl
from jax.experimental.pallas import tpu as pltpu
from jax.sharding import PartitionSpec as P

BS = 128
norm_eps = 1e-06
gelu_coef = 0.7978845608028654
beta_first = 0.9
beta_second = 0.95
adam_eps = 1e-08
learn_rate = 0.001
decay_rate = 0.1
update_count = 10
ROW_TILE = 16
VMEM_LIMIT = 60 * 1024 * 1024


def gelu(preact):
    tangent = jnp.tanh(gelu_coef * (preact + 0.044715 * preact * preact * preact))
    return 0.5 * preact * (1.0 + tangent)


def gelu_both(preact):
    square = preact * preact
    tangent = jnp.tanh(gelu_coef * (preact + 0.044715 * square * preact))
    half = 0.5 * (1.0 + tangent)
    slope = half + 0.5 * preact * (1.0 - tangent * tangent) * gelu_coef * (
        1.0 + 3.0 * 0.044715 * square
    )
    return (preact * half, slope)


def dot_plain(left, right):
    return jnp.dot(left, right, preferred_element_type=jnp.float32)


def dot_right_t(left, right):
    return lax.dot_general(left, right, (((1,), (1,)), ((), ())), preferred_element_type=jnp.float32)


def dot_left_t(left, right):
    return lax.dot_general(left, right, (((0,), (0,)), ((), ())), preferred_element_type=jnp.float32)


def fill_normed(x_ref, normed, base):
    rows, width = x_ref.shape

    def tile(i, carry):
        at = pl.multiple_of(i * ROW_TILE, ROW_TILE)
        wide = x_ref[pl.ds(at, ROW_TILE), :].astype(jnp.float32)
        factor = lax.rsqrt(jnp.mean(wide * wide, axis=-1, keepdims=True) + norm_eps)
        value = (wide * factor).astype(jnp.bfloat16)
        for b in range(width // BS):
            normed[b, pl.ds(base + at, ROW_TILE), :] = value[:, b * BS : (b + 1) * BS]
        return carry

    lax.fori_loop(0, rows // ROW_TILE, tile, 0)


def fill_split(x_ref, split, base):
    rows, width = x_ref.shape
    for b in range(width // BS):
        split[b, pl.ds(base, rows), :] = x_ref[:, b * BS : (b + 1) * BS]


def clear(ref):
    def one(i, carry):
        ref[i] = jnp.zeros(ref.shape[1:], ref.dtype)
        return carry

    lax.fori_loop(0, ref.shape[0], one, 0)


def accumulate(pattern, which, source, take, blocks, target, put, dot, base, rows):
    clear(target)

    def one(k, carry):
        left = source[pattern[which, k, take], pl.ds(base, rows), :]
        place = pattern[which, k, put]
        target[place] += dot(left, blocks[k])
        return carry

    lax.fori_loop(0, blocks.shape[0], one, 0, unroll=4)


def each(count, body):
    def one(i, carry):
        body(i)
        return carry

    lax.fori_loop(0, count, one, 0)


def forward_rows(x_ref, out_ref, pattern, weights, normed, wide_a, hidden, narrow):
    rows, width = x_ref.shape
    fill_normed(x_ref, normed, 0)
    accumulate(pattern, 0, normed, 0, weights.at[0], wide_a, 1, dot_plain, 0, rows)

    def act(c):
        hidden[c] = gelu(wide_a[c]).astype(jnp.bfloat16)

    each(wide_a.shape[0], act)
    accumulate(pattern, 1, hidden, 0, weights.at[1], narrow, 1, dot_plain, 0, rows)
    for b in range(width // BS):
        cols = slice(b * BS, (b + 1) * BS)
        out_ref[:, cols] = (x_ref[:, cols].astype(jnp.float32) + narrow[b]).astype(jnp.bfloat16)


def backward_rows(x_ref, cot_ref, out_ref, pattern, weights, normed, wide_a, wide_b, hidden, narrow):
    rows, width = x_ref.shape
    fill_normed(x_ref, normed, 0)
    accumulate(pattern, 0, normed, 0, weights.at[0], wide_a, 1, dot_plain, 0, rows)
    fill_split(cot_ref, normed, 0)
    accumulate(pattern, 1, normed, 1, weights.at[1], wide_b, 0, dot_right_t, 0, rows)

    def act(c):
        hidden[c] = (wide_b[c] * gelu_both(wide_a[c])[1]).astype(jnp.bfloat16)

    each(wide_a.shape[0], act)
    accumulate(pattern, 0, hidden, 1, weights.at[0], narrow, 0, dot_right_t, 0, rows)

    def tile(i):
        at = pl.multiple_of(i * ROW_TILE, ROW_TILE)
        wide = x_ref[pl.ds(at, ROW_TILE), :].astype(jnp.float32)
        factor = lax.rsqrt(jnp.mean(wide * wide, axis=-1, keepdims=True) + norm_eps)
        grad = jnp.concatenate(
            [narrow[b, pl.ds(at, ROW_TILE), :] for b in range(width // BS)], axis=-1
        )
        coupling = jnp.mean(wide * grad, axis=-1, keepdims=True)
        upstream = cot_ref[pl.ds(at, ROW_TILE), :].astype(jnp.float32)
        value = upstream + factor * grad - wide * (factor * factor * factor * coupling)
        out_ref[pl.ds(at, ROW_TILE), :] = value.astype(jnp.bfloat16)

    each(rows // ROW_TILE, tile)


def wide_shape(rows, blocks, dtype):
    return pltpu.VMEM((blocks, rows, BS), dtype)


def weight_spec(weights, step_copy):
    return pl.BlockSpec(
        (None,) + weights.shape[1:],
        lambda i, copies: (step_copy(i, copies), 0, 0, 0, 0),
    )


def pattern_spec(pattern, step_copy):
    return pl.BlockSpec(
        (None,) + pattern.shape[1:],
        lambda i, copies: (step_copy(i, copies), 0, 0, 0),
        memory_space=pltpu.SMEM,
    )


def whole_spec(array):
    return pl.BlockSpec(array.shape, lambda i, copies: (0,) * len(array.shape))


def rows_shape(array):
    return jax.ShapeDtypeStruct(array.shape, jnp.bfloat16)


def run_steps(kernel, copies, step_copy, step_total, pattern, weights, rows_in, outs, scratch, name):
    grid_spec = pltpu.PrefetchScalarGridSpec(
        num_scalar_prefetch=1,
        grid=(step_total,),
        in_specs=[pattern_spec(pattern, step_copy), weight_spec(weights, step_copy)]
        + [whole_spec(r) for r in rows_in],
        out_specs=[whole_spec(o) for o in outs],
        scratch_shapes=scratch,
    )
    return pl.pallas_call(
        kernel,
        grid_spec=grid_spec,
        out_shape=outs,
        name=name,
        compiler_params=pltpu.CompilerParams(
            dimension_semantics=("arbitrary",), vmem_limit_bytes=VMEM_LIMIT
        ),
    )(copies, pattern, weights, *rows_in)


def forward_call(x, copies, start, total, pattern, weights, ff_blocks):
    rows, width = x.shape

    def kernel(copies_ref, pattern_ref, weights_ref, x_ref, *rest):
        outs, (normed, wide_a, hidden, narrow) = rest[:total], rest[total:]
        for step in range(total):

            @pl.when(pl.program_id(0) == step)
            def run(step=step):
                source = x_ref if step == 0 else outs[step - 1]
                forward_rows(
                    source, outs[step], pattern_ref, weights_ref, normed, wide_a, hidden, narrow
                )

    scratch = [
        wide_shape(rows, width // BS, jnp.bfloat16),
        wide_shape(rows, ff_blocks, jnp.float32),
        wide_shape(rows, ff_blocks, jnp.bfloat16),
        wide_shape(rows, width // BS, jnp.float32),
    ]
    return run_steps(
        kernel, copies, lambda i, c: c[start + i], total, pattern, weights, [x],
        [rows_shape(x)] * total, scratch, "forward"
    )


def backward_call(xs, cot, copies, start, pattern, weights, ff_blocks):
    rows, width = cot.shape
    total = len(xs)

    def kernel(copies_ref, pattern_ref, weights_ref, *rest):
        inputs, cot_ref, rest = rest[:total], rest[total], rest[total + 1 :]
        outs, (normed, wide_a, wide_b, hidden, narrow) = rest[:total], rest[total:]
        for step in range(total):

            @pl.when(pl.program_id(0) == step)
            def run(step=step):
                upstream = cot_ref if step == 0 else outs[step - 1]
                backward_rows(
                    inputs[step], upstream, outs[step], pattern_ref, weights_ref,
                    normed, wide_a, wide_b, hidden, narrow
                )

    scratch = [
        wide_shape(rows, width // BS, jnp.bfloat16),
        wide_shape(rows, ff_blocks, jnp.float32),
        wide_shape(rows, ff_blocks, jnp.float32),
        wide_shape(rows, ff_blocks, jnp.bfloat16),
        wide_shape(rows, width // BS, jnp.float32),
    ]
    return run_steps(
        kernel, copies, lambda i, c: c[start - i], total, pattern, weights, list(xs) + [cot],
        [rows_shape(cot)] * total, scratch, "backward"
    )


def turn_call(x, targets, copies, pattern, weights, ff_blocks):
    rows, width = x.shape

    def kernel(copies_ref, pattern_ref, weights_ref, x_ref, target_ref, residue, out,
               normed, wide_a, wide_b, hidden, narrow):
        forward_rows(x_ref, residue, pattern_ref, weights_ref, normed, wide_a, hidden, narrow)
        for b in range(width // BS):
            cols = slice(b * BS, (b + 1) * BS)
            difference = residue[:, cols].astype(jnp.float32) - target_ref[:, cols].astype(jnp.float32)
            residue[:, cols] = difference.astype(jnp.bfloat16)
        backward_rows(
            x_ref, residue, out, pattern_ref, weights_ref, normed, wide_a, wide_b, hidden, narrow
        )

    scratch = [
        wide_shape(rows, width // BS, jnp.bfloat16),
        wide_shape(rows, ff_blocks, jnp.float32),
        wide_shape(rows, ff_blocks, jnp.float32),
        wide_shape(rows, ff_blocks, jnp.bfloat16),
        wide_shape(rows, width // BS, jnp.float32),
    ]
    return run_steps(
        kernel, copies, lambda i, c: c[1], 1, pattern, weights, [x, targets],
        [rows_shape(x)] * 2, scratch, "turn"
    )


def grads_call(xs, cots, copies, pattern, weights, ff_blocks, shares):
    rows, width = xs[0].shape
    parts = len(xs)
    block_total = weights.shape[2]
    share_rows = BS // shares

    def kernel(copies_ref, pattern_ref, weights_ref, *rest):
        inputs, upstreams, out = rest[:parts], rest[parts : 2 * parts], rest[2 * parts]
        normed, split, wide_a, wide_b, hidden, grad_pre = rest[2 * parts + 1 :]
        for part in range(parts):
            base = part * rows
            fill_normed(inputs[part], normed, base)
            fill_split(upstreams[part], split, base)
            accumulate(
                pattern_ref, 0, normed, 0, weights_ref.at[0], wide_a, 1, dot_plain, base, rows
            )
            accumulate(
                pattern_ref, 1, split, 1, weights_ref.at[1], wide_b, 0, dot_right_t, base, rows
            )

            def act(c):
                value, slope = gelu_both(wide_a[c])
                hidden[c, pl.ds(base, rows), :] = value.astype(jnp.bfloat16)
                grad_pre[c, pl.ds(base, rows), :] = (wide_b[c] * slope).astype(jnp.bfloat16)

            each(wide_a.shape[0], act)

        def one(k, carry):
            up = dot_left_t(
                normed[pattern_ref[0, k, 0]], grad_pre[pattern_ref[0, k, 1]]
            ).astype(jnp.bfloat16)
            down = dot_left_t(
                hidden[pattern_ref[1, k, 0]], split[pattern_ref[1, k, 1]]
            ).astype(jnp.bfloat16)
            for share in range(shares):
                span = slice(share * share_rows, (share + 1) * share_rows)
                out[share, 0, k] = up[span]
                out[share, 1, k] = down[span]
            return carry

        lax.fori_loop(0, block_total, one, 0, unroll=2)

    all_rows = rows * parts
    scratch = [
        wide_shape(all_rows, width // BS, jnp.bfloat16),
        wide_shape(all_rows, width // BS, jnp.bfloat16),
        wide_shape(rows, ff_blocks, jnp.float32),
        wide_shape(rows, ff_blocks, jnp.float32),
        wide_shape(all_rows, ff_blocks, jnp.bfloat16),
        wide_shape(all_rows, ff_blocks, jnp.bfloat16),
    ]
    out = jax.ShapeDtypeStruct((shares, 2, block_total, share_rows, BS), jnp.bfloat16)
    return run_steps(
        kernel, copies, lambda i, c: 0, 1, pattern, weights, list(xs) + list(cots),
        [out], scratch, "grads"
    )[0]


def adam_update(grad_sum, master, moment, variance, token_total):
    gradient = grad_sum / token_total
    moment_next = beta_first * moment + (1.0 - beta_first) * gradient
    variance_next = beta_second * variance + (1.0 - beta_second) * gradient * gradient
    corrected = moment_next / (1.0 - beta_first**update_count)
    spread = jnp.sqrt(variance_next / (1.0 - beta_second**update_count))
    step_direction = corrected / (spread + adam_eps)
    return (step_direction, master - learn_rate * (step_direction + decay_rate * master))


def shards(ff_blocks, tokens, targets, weights, pattern, master, moment, variance):
    section = lax.axis_index("section")
    sections = lax.axis_size("section")
    shares = lax.axis_size("dp")
    groups = sections // 2
    micro, rows_each, width = tokens.shape[1:]
    rows = micro * rows_each
    half = rows // 2
    high_member = (section >= groups).astype(jnp.int32)
    group = jnp.minimum(section, sections - 1 - section)
    copies = jnp.stack([high_member, 1 - high_member])
    weights, pattern = weights[0], pattern[0]

    def own_stream(array):
        return lax.dynamic_index_in_dim(array, high_member, 0, keepdims=False).reshape(rows, width)

    mirror = lambda i: sections - 1 - i
    straight = [(i, i + 1) for i in range(groups - 1)]
    straight += [(mirror(i), mirror(j)) for i, j in straight]
    crossed = [(i, mirror(i + 1)) for i in range(groups - 1)]
    crossed += [(mirror(i), mirror(j)) for i, j in crossed]

    def hop(x, inward):
        turned = lambda pairs: pairs if inward else [(j, i) for i, j in pairs]
        return jnp.concatenate(
            [
                lax.ppermute(x[:half], "section", turned(straight)),
                lax.ppermute(x[half:], "section", turned(crossed)),
            ]
        )

    def swap(x):
        return lax.ppermute(x, "section", [(i, mirror(i)) for i in range(sections)])

    def pick(at_group, fresh, kept):
        return jnp.where(group == at_group, fresh, kept)

    current = own_stream(tokens)
    x_low = current
    for i in range(groups - 1):
        (current,) = forward_call(current, copies, 0, 1, pattern, weights, ff_blocks)
        current = hop(current, True)
        x_low = pick(i + 1, current, x_low)
    if groups > 1:
        x_high, current = forward_call(current, copies, 0, 2, pattern, weights, ff_blocks)
        for i in reversed(range(groups - 1)):
            current = hop(current, False)
            x_high = pick(i, current, x_high)
            if i > 0:
                (current,) = forward_call(current, copies, 1, 1, pattern, weights, ff_blocks)
    residue, current = turn_call(x_high, own_stream(targets), copies, pattern, weights, ff_blocks)
    cot_high = residue
    for i in range(1, groups):
        current = hop(current, True)
        cot_high = pick(i, current, cot_high)
        if i < groups - 1:
            (current,) = backward_call([x_high], current, copies, 1, pattern, weights, ff_blocks)
    cot_low, current = backward_call(
        [x_high, x_low], cot_high, copies, 1, pattern, weights, ff_blocks
    )
    for i in reversed(range(groups - 1)):
        current = hop(current, False)
        cot_low = pick(i, current, cot_low)
        if i > 0:
            (current,) = backward_call([x_low], cot_low, copies, 0, pattern, weights, ff_blocks)

    is_high = high_member == 1
    x_other = swap(jnp.where(is_high, x_low, x_high))
    cot_other = swap(jnp.where(is_high, cot_low, cot_high))
    x_own = jnp.where(is_high, x_high, x_low)
    cot_own = jnp.where(is_high, cot_high, cot_low)
    grads = grads_call(
        [x_own, x_other], [cot_own, cot_other], copies, pattern, weights, ff_blocks, shares
    )
    share = lax.psum_scatter(grads, "dp", scatter_dimension=0, tiled=True)[0].astype(jnp.float32)
    token_total = 2 * rows * shares
    step_direction, master_next = adam_update(share, master[0], moment[0], variance[0], token_total)
    return (step_direction[None], master_next[None])


def solution(mesh):
    rows_split = P(None, None, "dp", None)
    by_section = P("section", None, None, "dp", None)
    return jax.shard_map(
        functools.partial(shards, FF_BLOCKS),
        mesh=mesh,
        in_specs=(
            rows_split,
            rows_split,
            P("section", None, None, None, None, None),
            P("section", None, None, None, None),
            by_section,
            by_section,
            by_section,
        ),
        out_specs=(by_section, by_section),
        check_vma=False,
    )


FF_BLOCKS = 8192 // BS
```

time: 1660 us -> 430 us (0.26); the launches traced: 1630 us -> 430 us
  other arithmetic: 655 us -> 12.4 us
  local copies, waits for them, and re-layouts: 324 us -> 13.2 us
  Pallas kernels: 0 us -> 225 us
  starting transfers between devices: 233 us -> 17.5 us
  matrix products: 196 us -> 0 us
  loops' own time: 34.7 us -> 0 us
  waiting for transfers between devices: 176 us -> 147 us
    scatter-add x32 -> x0, other arithmetic: 320 us -> none  [the longest x16 160 us: sparse_transposed(): summed = jax.ops.segment_sum(product, put_index, num_segments=out_blocks)]
    pallas_call x0 -> x5, Pallas kernels: none -> 225 us  [run_steps(): pl.pallas_call(kernel, grid_spec=grid_spec, out_shape=outs, name=name, co...]
    ppermute x30 -> x10, starting transfers between devices: 233 us -> 17.5 us  [the longest x4 9.03 us: hop(): lax.ppermute(x[:half], 'section', turned(straight))]
    scatter x91 -> x0, other arithmetic: 205 us -> none  [keep_slot(): return store.at[stream, slot_index].set(jnp.where(active, value, previous))]
    dot_general x36 -> x0, matrix products: 196 us -> none  [the longest x16 95.7 us: sparse_transposed(): jnp.einsum('rkb,kab->kra', picked, blocks, preferred_element_type=jnp.flo...]
    dynamic_slice x112 -> x2, local copies, waits for them, and re-layouts: 106 us -> 3.36 us  [own_stream(): lax.dynamic_index_in_dim(array, high_member, 0, keepdims=False)]
    convert_element_type x56 -> x0, other arithmetic: 83.2 us -> none  [the longest x16 42.8 us: layer_backward(): grad_preact = (grad_hidden * gelu_slope(preact)).astype(jnp.bfloat16)]
    gather x40 -> x0, local copies, waits for them, and re-layouts: 83.1 us -> none  [the longest x16 22 us: sparse_transposed(): picked = jnp.take(left_rows.reshape(row_count, -1, BS), take_index, axis=1)]
  transfers between devices with their start and end apart: 32 -> 11, of which waited for: 5 -> 10; matrix products, arithmetic and copies ran while one was open for 39% -> 1% of each run, Pallas kernels for 0% -> 0%
where the time goes in v1:
time: 430 us
  Pallas kernels  225 us (52%)
  waiting for transfers between devices  147 us (34%)
  starting transfers between devices  17.5 us (4%)
  between operations  14.2 us (3%)
  local copies, waits for them, and re-layouts  13.2 us (3%)
  other arithmetic  12.4 us (3%)
    pallas_call x5, Pallas kernels, run_steps(): pl.pallas_call(kernel, grid_spec=grid_spec, out_shape=outs, name=name, co...  225 us
    reduce_scatter x1, waiting for transfers between devices, shards(): lax.psum_scatter(grads, 'dp', scatter_dimension=0, tiled=True)[0]  70.2 us
    ppermute x4, waiting for transfers between devices, hop(): lax.ppermute(x[:half], 'section', turned(straight))  35 us
    ppermute x4, waiting for transfers between devices, hop(): lax.ppermute(x[half:], 'section', turned(crossed))  21.7 us
    ppermute x2, waiting for transfers between devices, swap(): return lax.ppermute(x, 'section', [(i, mirror(i)) for i in range(sections)])  20.4 us
    ppermute x4, starting transfers between devices, hop(): lax.ppermute(x[:half], 'section', turned(straight))  9.03 us
  transfers between devices with their start and end apart: 11, of which 10 were waited for; matrix products, arithmetic and copies ran while one was open for 1% of the time, Pallas kernels for 0%

profile of v1, /device:TPU:0, one launch (start us, length us, event | category | flops | bytes accessed | tf_op | source)
XLA Modules:
  0.0 429.6 jit_solution(13577037275133690221)
XLA Ops:
  7.2 0.0 copy-start
  7.2 0.0 reduce-scatter.2.cloned.1.call-start
  7.2 1.6 copy.9
  8.9 0.6 pad_add_fusion.copies_ref
  9.4 0.0 copy-done
  9.4 1.0 constant_dynamic-slice_fusion.1
  10.4 20.7 %forward.2 = bf16[224,2048]{1,0:T(8,128)(2,1)} custom-call(s32[2]{0:T(128)} %pad_add_fusion.copies_ref, s32[2,2,96,2]{3,2,1,0:T(8,128)} %bitcast.14, bf16[2,2,96,128,128]{4,3,2,1,0:T(8,128)(2,1)} %bitcast.8, bf16[224,2048]{1,0:T(8,128)(2,1)} %bitcast.13), custom_call_target="tpu_custom_call" | custom-call | tf_op jit(solution)/shard_map/forward/pallas_call | solution.py:178
  31.1 1.2 fusion.12
  32.4 4.9 %collective-permute-start = (bf16[112,2048]{1,0:T(8,128)(2,1)S(1)}, bf16[112,2048]{1,0:T(8,128)(2,1)S(1)}, u32[]{:S(2)}, u32[]{:S(2)}) collective-permute-start(bf16[112,2048]{1,0:T(8,128)(2,1)S(1)} %get-tuple-element.28), channel_id=1, source_target_pairs={{0,8},{24,16},{1,9},{25,17},{2,10},{26,18},{3,11},{27,19},{4,12},{... | collective-permute-start | bytes 1376264 | tf_op jit(solution)/shard_map/ppermute | solution.py:366
  37.3 1.3 collective-permute-start.1
  38.6 8.4 %collective-permute-done = bf16[112,2048]{1,0:T(8,128)(2,1)S(1)} collective-permute-done((bf16[112,2048]{1,0:T(8,128)(2,1)S(1)}, bf16[112,2048]{1,0:T(8,128)(2,1)S(1)}, u32[]{:S(2)}, u32[]{:S(2)}) %collective-permute-start) | collective-permute-done | bytes 458784 | tf_op jit(solution)/shard_map/ppermute | solution.py:366
  47.0 1.3 collective-permute-done.1
  48.4 0.0 copy-start.5
  48.4 0.9 copy-done.5
  49.3 37.2 %forward.3 = (bf16[224,2048]{1,0:T(8,128)(2,1)}, bf16[224,2048]{1,0:T(8,128)(2,1)}) custom-call(s32[2]{0:T(128)} %pad_add_fusion.copies_ref, s32[2,2,96,2]{3,2,1,0:T(8,128)} %bitcast.15, bf16[2,2,96,128,128]{4,3,2,1,0:T(8,128)(2,1)} %bitcast.9, bf16[224,2048]{1,0:T(8,128)(2,1)} %copy-done.5), custom_call_target="tpu_custom_call" | custom-call | tf_op jit(solution)/shard_map/forward/pallas_call | solution.py:178
  86.5 2.3 fusion.11
  88.8 1.3 collective-permute-start.2
  90.1 1.3 collective-permute-start.3
  91.4 0.0 copy-start.6
  91.4 2.3 constant_dynamic-slice_fusion
  93.7 8.7 %collective-permute-done.2 = bf16[112,2048]{1,0:T(8,128)(2,1)S(1)} collective-permute-done((bf16[112,2048]{1,0:T(8,128)(2,1)}, bf16[112,2048]{1,0:T(8,128)(2,1)S(1)}, u32[]{:S(2)}, u32[]{:S(2)}) %collective-permute-start.2) | collective-permute-done | bytes 458784 | tf_op jit(solution)/shard_map/ppermute | solution.py:366
  102.4 1.4 collective-permute-done.3
  103.8 0.0 copy-done.6
  103.8 3.1 broadcast_select_fusion.3
  106.9 47.9 %turn.1 = (bf16[224,2048]{1,0:T(8,128)(2,1)}, bf16[224,2048]{1,0:T(8,128)(2,1)}) custom-call(s32[2]{0:T(128)} %pad_add_fusion.copies_ref, s32[2,2,96,2]{3,2,1,0:T(8,128)} %bitcast.16, bf16[2,2,96,128,128]{4,3,2,1,0:T(8,128)(2,1)} %bitcast.10, bf16[224,2048]{1,0:T(8,128)(2,1)} %get-tuple-element.18.x_ref.rest_0_, bf16[224,2048]{1,0:T(8,128)(2,1)} %bitcast.19), custom_call_target="tpu_custom_call" | custom-call | tf_op jit(solution)/shard_map/turn/pallas_call | solution.py:178
  154.8 1.3 fusion.10
  156.2 1.6 collective-permute-start.5
  157.7 1.3 collective-permute-start.6
  159.0 6.9 %collective-permute-done.5 = bf16[112,2048]{1,0:T(8,128)(2,1)S(1)} collective-permute-done((bf16[112,2048]{1,0:T(8,128)(2,1)S(1)}, bf16[112,2048]{1,0:T(8,128)(2,1)S(1)}, u32[]{:S(2)}, u32[]{:S(2)}) %collective-permute-start.5) | collective-permute-done | bytes 458784 | tf_op jit(solution)/shard_map/ppermute | solution.py:366
  165.9 1.3 collective-permute-done.6
  167.2 1.3 maximum_select_fusion.1.rest_2_
  168.5 58.2 %backward.1 = (bf16[224,2048]{1,0:T(8,128)(2,1)}, bf16[224,2048]{1,0:T(8,128)(2,1)}) custom-call(s32[2]{0:T(128)} %pad_add_fusion.copies_ref, s32[2,2,96,2]{3,2,1,0:T(8,128)} %bitcast.17, bf16[2,2,96,128,128]{4,3,2,1,0:T(8,128)(2,1)} %bitcast.11, bf16[224,2048]{1,0:T(8,128)(2,1)} %get-tuple-element.18.x_ref.rest_0_, ...), custom_call_target="tpu_custom_call" | custom-call | tf_op jit(solution)/shard_map/backward/pallas_call | solution.py:178
  226.8 1.4 fusion.9
  228.1 1.3 collective-permute-start.7
  229.4 1.3 collective-permute-start.8
  230.7 1.6 collective-permute-start.4
  232.4 11.1 %collective-permute-done.7 = bf16[112,2048]{1,0:T(8,128)(2,1)S(1)} collective-permute-done((bf16[112,2048]{1,0:T(8,128)(2,1)S(1)}, bf16[112,2048]{1,0:T(8,128)(2,1)S(1)}, u32[]{:S(2)}, u32[]{:S(2)}) %collective-permute-start.7) | collective-permute-done | bytes 458784 | tf_op jit(solution)/shard_map/ppermute | solution.py:366
  243.4 17.7 %collective-permute-done.8 = bf16[112,2048]{1,0:T(8,128)(2,1)S(1)} collective-permute-done((bf16[112,2048]{1,0:T(8,128)(2,1)S(1)}, bf16[112,2048]{1,0:T(8,128)(2,1)S(1)}, u32[]{:S(2)}, u32[]{:S(2)}) %collective-permute-start.8) | collective-permute-done | bytes 458784 | tf_op jit(solution)/shard_map/ppermute | solution.py:367
  261.1 1.5 broadcast_select_fusion.1
  262.5 1.6 collective-permute-start.9
  264.1 1.0 broadcast_select_fusion.4.rest_0_
  265.2 0.0 collective-permute-done.4.rest_1_
  265.2 20.4 %collective-permute-done.9.rest_3_ = bf16[224,2048]{1,0:T(8,128)(2,1)S(1)} collective-permute-done((bf16[224,2048]{1,0:T(8,128)(2,1)S(1)}, bf16[224,2048]{1,0:T(8,128)(2,1)S(1)}, u32[]{:S(2)}, u32[]{:S(2)}) %collective-permute-start.9) | collective-permute-done | bytes 917536 | tf_op jit(solution)/shard_map/ppermute | solution.py:372
  285.5 1.0 copy-done.13
  286.5 60.9 %grads.1 = bf16[8,2,96,16,128]{4,3,2,1,0:T(8,128)(2,1)} custom-call(s32[2]{0:T(128)} %pad_add_fusion.copies_ref, s32[2,2,96,2]{3,2,1,0:T(8,128)} %bitcast.18, bf16[2,2,96,128,128]{4,3,2,1,0:T(8,128)(2,1)} %bitcast.12, bf16[224,2048]{1,0:T(8,128)(2,1)} %broadcast_select_fusion.4.rest_0_, bf16[224,2048]{1,0:T(8,128)(2,1)} %copy-done.12, ...), custom_call_target="tpu_custom_call" | custom-call | tf_op jit(solution)/shard_map/grads/pallas_call | solution.py:178
  347.4 0.0 reduce-scatter.2.cloned.1.call-update
  347.4 70.2 %reduce-scatter.2.cloned.1.call-done = bf16[1,2,96,16,128]{4,3,2,1,0:T(8,128)(2,1)} async-done(((bf16[8,2,96,16,128]{4,3,2,1,0:T(8,128)(2,1)}), bf16[1,2,96,16,128]{4,3,2,1,0:T(8,128)(2,1)}) %reduce-scatter.2.cloned.1.call-update) | async-done | bytes 786448 | tf_op jit(solution)/shard_map/reduce_scatter | solution.py:414
  417.7 5.1 %multiply_subtract_fusion = (f32[1,2,96,16,128]{4,3,2,1,0:T(8,128)}, f32[1,2,96,16,128]{4,3,2,1,0:T(8,128)}) fusion(f32[1,2,96,16,128]{4,3,2,1,0:T(8,128)S(1)} %copy-done.7, f32[1,2,96,16,128]{4,3,2,1,0:T(8,128)} %param.13, bf16[1,2,96,16,128]{4,3,2,1,0:T(8,128)(2,1)} %reduce-scatter.2.cloned.1.call-done, f32[1,2,96,16,128]{4,3,2,1,0:T(8,128)} %param.12), kind=kLoop, calls=%fused_computation.11 | loop fusion | flops 6684672 | bytes 8650752 | tf_op jit(solution)/shard_map/sub | solution.py:337
  (23 shorter events, 0.1 us)
Async XLA Ops:
  7.2 2.2 copy-start
  7.2 410.5 %reduce-scatter.2.cloned.1.call-start = ((), (), s32[]{:S(2)}) async-start(), calls=%async_computation.1 | async-start | bytes 7077888 | tf_op jit(solution)/shard_map/reduce_scatter | solution.py:414
  32.4 14.6 %collective-permute-start = (bf16[112,2048]{1,0:T(8,128)(2,1)S(1)}, bf16[112,2048]{1,0:T(8,128)(2,1)S(1)}, u32[]{:S(2)}, u32[]{:S(2)}) collective-permute-start(bf16[112,2048]{1,0:T(8,128)(2,1)S(1)} %get-tuple-element.28), channel_id=1, source_target_pairs={{0,8},{24,16},{1,9},{25,17},{2,10},{26,18},{3,11},{27,19},{4,12},{... | collective-permute-start | bytes 1376264 | tf_op jit(solution)/shard_map/ppermute | solution.py:366
  37.3 11.1 %collective-permute-start.1 = (bf16[112,2048]{1,0:T(8,128)(2,1)S(1)}, bf16[112,2048]{1,0:T(8,128)(2,1)S(1)}, u32[]{:S(2)}, u32[]{:S(2)}) collective-permute-start(bf16[112,2048]{1,0:T(8,128)(2,1)S(1)} %get-tuple-element.27), channel_id=1, source_target_pairs={{0,16},{24,8},{1,17},{25,9},{2,18},{26,10},{3,19},{27,11},{4,20},{... | collective-permute-start | bytes 1376264 | tf_op jit(solution)/shard_map/ppermute | solution.py:367
  48.4 0.9 copy-start.5
  86.5 17.3 %copy-start.2 = (bf16[1,4,56,2048]{3,2,1,0:T(8,128)(2,1)S(1)}, bf16[1,4,56,2048]{3,2,1,0:T(8,128)(2,1)}, u32[]{:S(2)}) copy-start(bf16[1,4,56,2048]{3,2,1,0:T(8,128)(2,1)} %constant_dynamic-slice_fusion.1) | copy-start | bytes 2752516
  88.8 13.7 %collective-permute-start.2 = (bf16[112,2048]{1,0:T(8,128)(2,1)}, bf16[112,2048]{1,0:T(8,128)(2,1)S(1)}, u32[]{:S(2)}, u32[]{:S(2)}) collective-permute-start(bf16[112,2048]{1,0:T(8,128)(2,1)} %get-tuple-element.25), channel_id=1, source_target_pairs={{8,0},{16,24},{9,1},{17,25},{10,2},{18,26},{11,3},{19,27},{12,4},{... | collective-permute-start | bytes 1376264 | tf_op jit(solution)/shard_map/ppermute | solution.py:366
  90.1 13.8 %collective-permute-start.3 = (bf16[112,2048]{1,0:T(8,128)(2,1)}, bf16[112,2048]{1,0:T(8,128)(2,1)}, u32[]{:S(2)}, u32[]{:S(2)}) collective-permute-start(bf16[112,2048]{1,0:T(8,128)(2,1)} %get-tuple-element.26), channel_id=1, source_target_pairs={{16,0},{8,24},{17,1},{9,25},{18,2},{10,26},{19,3},{11,27},{20,4},{... | collective-permute-start | bytes 1376264 | tf_op jit(solution)/shard_map/ppermute | solution.py:367
  91.4 12.5 %copy-start.6 = (bf16[224,2048]{1,0:T(8,128)(2,1)S(1)}, bf16[224,2048]{1,0:T(8,128)(2,1)}, u32[]{:S(2)}) copy-start(bf16[224,2048]{1,0:T(8,128)(2,1)} %copy-done.5) | copy-start | bytes 2752516
  91.4 12.4 %copy-start.11 = (bf16[224,2048]{1,0:T(8,128)(2,1)S(1)}, bf16[224,2048]{1,0:T(8,128)(2,1)}, u32[]{:S(2)}) copy-start(bf16[224,2048]{1,0:T(8,128)(2,1)} %get-tuple-element.9) | copy-start | bytes 2752516
  154.8 12.4 %copy-start.9 = (bf16[224,2048]{1,0:T(8,128)(2,1)S(1)}, bf16[224,2048]{1,0:T(8,128)(2,1)}, u32[]{:S(2)}) copy-start(bf16[224,2048]{1,0:T(8,128)(2,1)} %get-tuple-element.11) | copy-start | bytes 2752516
  156.2 9.8 %collective-permute-start.5 = (bf16[112,2048]{1,0:T(8,128)(2,1)S(1)}, bf16[112,2048]{1,0:T(8,128)(2,1)S(1)}, u32[]{:S(2)}, u32[]{:S(2)}) collective-permute-start(bf16[112,2048]{1,0:T(8,128)(2,1)S(1)} %get-tuple-element.23), channel_id=1, source_target_pairs={{0,8},{24,16},{1,9},{25,17},{2,10},{26,18},{3,11},{27,19},{4,12},{... | collective-permute-start | bytes 1376264 | tf_op jit(solution)/shard_map/ppermute | solution.py:366
  157.7 9.5 %collective-permute-start.6 = (bf16[112,2048]{1,0:T(8,128)(2,1)S(1)}, bf16[112,2048]{1,0:T(8,128)(2,1)S(1)}, u32[]{:S(2)}, u32[]{:S(2)}) collective-permute-start(bf16[112,2048]{1,0:T(8,128)(2,1)S(1)} %get-tuple-element.24), channel_id=1, source_target_pairs={{0,16},{24,8},{1,17},{25,9},{2,18},{26,10},{3,19},{27,11},{4,20},{... | collective-permute-start | bytes 1376264 | tf_op jit(solution)/shard_map/ppermute | solution.py:367
  168.5 62.2 %copy-start.10 = (bf16[224,2048]{1,0:T(8,128)(2,1)S(1)}, bf16[224,2048]{1,0:T(8,128)(2,1)}, u32[]{:S(2)}) copy-start(bf16[224,2048]{1,0:T(8,128)(2,1)} %get-tuple-element.16) | copy-start | bytes 2752516
  226.8 34.3 %copy-start.3 = (bf16[224,2048]{1,0:T(8,128)(2,1)S(1)}, bf16[224,2048]{1,0:T(8,128)(2,1)}, u32[]{:S(2)}) copy-start(bf16[224,2048]{1,0:T(8,128)(2,1)} %maximum_select_fusion.1.rest_2_) | copy-start | bytes 2752516
  226.8 34.3 %copy-start.8 = (bf16[224,2048]{1,0:T(8,128)(2,1)S(1)}, bf16[224,2048]{1,0:T(8,128)(2,1)}, u32[]{:S(2)}) copy-start(bf16[224,2048]{1,0:T(8,128)(2,1)} %get-tuple-element.13) | copy-start | bytes 2752516
  228.1 15.3 %collective-permute-start.7 = (bf16[112,2048]{1,0:T(8,128)(2,1)S(1)}, bf16[112,2048]{1,0:T(8,128)(2,1)S(1)}, u32[]{:S(2)}, u32[]{:S(2)}) collective-permute-start(bf16[112,2048]{1,0:T(8,128)(2,1)S(1)} %get-tuple-element.21), channel_id=1, source_target_pairs={{8,0},{16,24},{9,1},{17,25},{10,2},{18,26},{11,3},{19,27},{12,4},{... | collective-permute-start | bytes 1376264 | tf_op jit(solution)/shard_map/ppermute | solution.py:366
  229.4 31.6 %collective-permute-start.8 = (bf16[112,2048]{1,0:T(8,128)(2,1)S(1)}, bf16[112,2048]{1,0:T(8,128)(2,1)S(1)}, u32[]{:S(2)}, u32[]{:S(2)}) collective-permute-start(bf16[112,2048]{1,0:T(8,128)(2,1)S(1)} %get-tuple-element.22), channel_id=1, source_target_pairs={{16,0},{8,24},{17,1},{9,25},{18,2},{10,26},{19,3},{11,27},{20,4},{... | collective-permute-start | bytes 1376264 | tf_op jit(solution)/shard_map/ppermute | solution.py:367
  230.7 34.4 %collective-permute-start.4 = (bf16[224,2048]{1,0:T(8,128)(2,1)S(1)}, bf16[224,2048]{1,0:T(8,128)(2,1)S(1)}, u32[]{:S(2)}, u32[]{:S(2)}) collective-permute-start(bf16[224,2048]{1,0:T(8,128)(2,1)S(1)} %copy-done.10), channel_id=1, source_target_pairs={{0,24},{8,16},{16,8},{24,0},{1,25},{9,17},{17,9},{25,1},{2,26},{10... | collective-permute-start | bytes 2752520 | tf_op jit(solution)/shard_map/ppermute | solution.py:372
  261.1 3.1 copy-start.1
  261.1 3.1 copy-start.4
  262.5 23.0 %collective-permute-start.9 = (bf16[224,2048]{1,0:T(8,128)(2,1)S(1)}, bf16[224,2048]{1,0:T(8,128)(2,1)S(1)}, u32[]{:S(2)}, u32[]{:S(2)}) collective-permute-start(bf16[224,2048]{1,0:T(8,128)(2,1)S(1)} %get-tuple-element.19), channel_id=1, source_target_pairs={{0,24},{8,16},{16,8},{24,0},{1,25},{9,17},{17,9},{25,1},{2,26},{10... | collective-permute-start | bytes 2752520 | tf_op jit(solution)/shard_map/ppermute | solution.py:372
  265.2 21.4 %copy-start.12 = (bf16[224,2048]{1,0:T(8,128)(2,1)}, bf16[224,2048]{1,0:T(8,128)(2,1)S(1)}, u32[]{:S(2)}) copy-start(bf16[224,2048]{1,0:T(8,128)(2,1)S(1)} %collective-permute-done.4.rest_1_) | copy-start | bytes 2752516
  285.5 1.0 copy-start.13
  347.4 70.3 %copy-start.7 = (f32[1,2,96,16,128]{4,3,2,1,0:T(8,128)S(1)}, f32[1,2,96,16,128]{4,3,2,1,0:T(8,128)}, u32[]{:S(2)}) copy-start(f32[1,2,96,16,128]{4,3,2,1,0:T(8,128)} %param.11) | copy-start | bytes 4718596
Sparse Core Ops, SparseCore 0:
  347.5 70.0 reduce-scatter.1

commit v2 on v1

v2 whole, which is shorter than its diff:
```python
import functools

import jax
import jax.numpy as jnp
from jax import lax
from jax.experimental import pallas as pl
from jax.experimental.pallas import tpu as pltpu
from jax.sharding import PartitionSpec as P

BS = 128
FF_BLOCKS = 8192 // BS
norm_eps = 1e-06
gelu_coef = 0.7978845608028654
gelu_cubic = gelu_coef * 0.044715
beta_first = 0.9
beta_second = 0.95
adam_eps = 1e-08
learn_rate = 0.001
decay_rate = 0.1
update_count = 10
ROW_TILE = 16
VMEM_LIMIT = 60 * 1024 * 1024
UP_WIDE, DOWN_WIDE, DOWN_NARROW, UP_NARROW = range(4)
FIELDS = 9
FIRST, FIRST_TAKE, SECOND, SECOND_TAKE, PUT, EXTRA, EXTRA_TAKE, EXTRA_PUT, COUNT = range(FIELDS)


def block_lists(pattern):
    total = pattern.shape[2]
    up_row, up_col = pattern[:, 0, :, 0], pattern[:, 0, :, 1]
    down_row, down_col = pattern[:, 1, :, 0], pattern[:, 1, :, 1]
    key = jnp.stack([up_col, down_row, down_col, up_row], 1)
    take = jnp.stack([up_row, down_col, down_row, up_col], 1)
    order = jnp.arange(total, dtype=jnp.int32)
    before = order[None, :] < order[:, None]

    def count(mask):
        return jnp.sum(mask.astype(jnp.int32), axis=-1)

    same = key[..., None, :] == key[..., :, None]
    rank = count(same & before)
    even = rank % 2 == 0
    wide = (jnp.arange(4) < 2)[None, :, None]
    extra = rank >= 2
    extra_place = count(extra[..., None, :] & before)
    pair = count((key[..., None, :] < key[..., :, None]) & even[..., None, :]) + rank // 2
    place_first = jnp.where(wide, jnp.where(rank == 0, key, -1), jnp.where(even, pair, -1))
    place_second = jnp.where(wide, jnp.where(rank == 1, key, -1), jnp.where(even, -1, pair))
    place_extra = jnp.where(wide & extra, extra_place, -1)
    number = jnp.broadcast_to(order, key.shape)
    places = jnp.stack(
        [place_first] * 2 + [place_second] * 2 + [place_first] + [place_extra] * 3, 2
    )
    values = jnp.stack([number, take, number - total, take, key, number, take, key], 2)
    hit = places[..., None, :] == order[:, None]
    fields = jnp.sum(jnp.where(hit, values[..., None, :], 0), axis=-1)
    fields = fields + jnp.where(jnp.arange(8) == SECOND, total, 0)[:, None]
    counts = jnp.where(wide[..., 0], count(extra), count(even))
    counts = jnp.broadcast_to(counts[..., None, None], key.shape[:2] + (1, total))
    return jnp.concatenate([fields, counts], axis=2).astype(jnp.int32).reshape(-1)


class Lists:
    def __init__(self, ref, copy, total):
        self.ref, self.total = ref, total
        self.base = copy * (4 * FIELDS * total)

    def __call__(self, kind, field, index):
        return self.ref[self.base + ((kind * FIELDS + field) * self.total) + index]


def hidden_of(preact):
    inner = preact * (gelu_coef + gelu_cubic * (preact * preact))
    half = 0.5 * preact
    return half + half * jnp.tanh(inner)


def slope_of(preact):
    cubic = gelu_cubic * (preact * preact)
    tangent = jnp.tanh(preact * (gelu_coef + cubic))
    bend = preact * (gelu_coef + 3.0 * cubic)
    return (0.5 + 0.5 * tangent) * (1.0 + bend * (1.0 - tangent))


def both_of(preact):
    cubic = gelu_cubic * (preact * preact)
    tangent = jnp.tanh(preact * (gelu_coef + cubic))
    bend = preact * (gelu_coef + 3.0 * cubic)
    half = 0.5 + 0.5 * tangent
    return (preact * half, half * (1.0 + bend * (1.0 - tangent)))


def dot_plain(left, right):
    return jnp.dot(left, right, preferred_element_type=jnp.float32)


def dot_right_t(left, right):
    return lax.dot_general(left, right, (((1,), (1,)), ((), ())), preferred_element_type=jnp.float32)


def each(count, body, unroll=1):
    def one(i, carry):
        body(i)
        return carry

    lax.fori_loop(0, count, one, 0, unroll=unroll)


def fill_normed(x_ref, normed, base):
    rows, width = x_ref.shape

    def tile(i):
        at = pl.multiple_of(i * ROW_TILE, ROW_TILE)
        wide = x_ref[pl.ds(at, ROW_TILE), :].astype(jnp.float32)
        factor = lax.rsqrt(jnp.mean(wide * wide, axis=-1, keepdims=True) + norm_eps)
        value = (wide * factor).astype(jnp.bfloat16)
        for b in range(width // BS):
            normed[b, pl.ds(base + at, ROW_TILE), :] = value[:, b * BS : (b + 1) * BS]

    each(rows // ROW_TILE, tile)


def fill_split(x_ref, split, base):
    rows, width = x_ref.shape
    for b in range(width // BS):
        split[b, pl.ds(base, rows), :] = x_ref[:, b * BS : (b + 1) * BS]


def pair_product(source, blocks, lists, kind, p, transposed):
    left = jnp.concatenate(
        [source[lists(kind, FIRST_TAKE, p)], source[lists(kind, SECOND_TAKE, p)]], axis=1
    )
    one, two = blocks[lists(kind, FIRST, p)], blocks[lists(kind, SECOND, p)]
    if transposed:
        return dot_right_t(left, jnp.concatenate([one, two], axis=1))
    return dot_plain(left, jnp.concatenate([one, two], axis=0))


def wide_pass(source, blocks, lists, kind, sums, finish, transposed):
    def main(c):
        value = pair_product(source, blocks, lists, kind, c, transposed)
        sums[c] = value
        finish(c, value)

    each(sums.shape[0], main, 2)
    dot = dot_right_t if transposed else dot_plain

    def more(e):
        c = lists(kind, EXTRA_PUT, e)
        left = source[lists(kind, EXTRA_TAKE, e)]
        value = sums[c] + dot(left, blocks[lists(kind, EXTRA, e)])
        sums[c] = value
        finish(c, value)

    each(lists(kind, COUNT, 0), more)


def narrow_pass(source, blocks, lists, kind, sums, transposed):
    sums[...] = jnp.zeros(sums.shape, sums.dtype)

    def one(p):
        sums[lists(kind, PUT, p)] += pair_product(source, blocks, lists, kind, p, transposed)

    count = lists(kind, COUNT, 0)

    def two(i):
        one(2 * i)
        one(2 * i + 1)

    each(count // 2, two)

    @pl.when(count % 2 == 1)
    def last():
        one(count - 1)


def forward_rows(x_ref, out_ref, lists, weights, scratch, slopes=None):
    normed, sums, hidden, narrow = scratch
    rows, width = x_ref.shape
    fill_normed(x_ref, normed, 0)
    weights.wait(0)

    def finish(c, value):
        if slopes is None:
            hidden[c] = hidden_of(value).astype(jnp.bfloat16)
        else:
            value, slope = both_of(value)
            hidden[c] = value.astype(jnp.bfloat16)
            slopes[c] = slope

    wide_pass(normed, weights.blocks(0), lists, UP_WIDE, sums, finish, False)
    weights.wait(1)
    narrow_pass(hidden, weights.blocks(1), lists, DOWN_NARROW, narrow, False)
    for b in range(width // BS):
        cols = slice(b * BS, (b + 1) * BS)
        out_ref[:, cols] = (x_ref[:, cols].astype(jnp.float32) + narrow[b]).astype(jnp.bfloat16)


def slope_rows(x_ref, lists, weights, scratch, slopes):
    normed, sums, hidden, narrow = scratch
    fill_normed(x_ref, normed, 0)
    weights.wait(0)

    def finish(c, value):
        slopes[c] = slope_of(value)

    wide_pass(normed, weights.blocks(0), lists, UP_WIDE, sums, finish, False)
    weights.wait(1)


def backward_rows(x_ref, cot_ref, out_ref, lists, weights, scratch, slopes):
    normed, sums, hidden, narrow = scratch
    rows, width = x_ref.shape
    fill_split(cot_ref, normed, 0)

    def finish(c, value):
        hidden[c] = (value * slopes[c]).astype(jnp.bfloat16)

    wide_pass(normed, weights.blocks(1), lists, DOWN_WIDE, sums, finish, True)
    narrow_pass(hidden, weights.blocks(0), lists, UP_NARROW, narrow, True)

    def tile(i):
        at = pl.multiple_of(i * ROW_TILE, ROW_TILE)
        wide = x_ref[pl.ds(at, ROW_TILE), :].astype(jnp.float32)
        factor = lax.rsqrt(jnp.mean(wide * wide, axis=-1, keepdims=True) + norm_eps)
        grad = jnp.concatenate(
            [narrow[b, pl.ds(at, ROW_TILE), :] for b in range(width // BS)], axis=-1
        )
        coupling = jnp.mean(wide * grad, axis=-1, keepdims=True)
        upstream = cot_ref[pl.ds(at, ROW_TILE), :].astype(jnp.float32)
        value = upstream + factor * grad - wide * (factor * factor * factor * coupling)
        out_ref[pl.ds(at, ROW_TILE), :] = value.astype(jnp.bfloat16)

    each(rows // ROW_TILE, tile)


class Weights:
    def __init__(self, hbm, local, sems, slot, copy):
        self.hbm, self.local, self.sems, self.slot, self.copy = hbm, local, sems, slot, copy

    def move(self, part):
        total = self.hbm.shape[2]
        return pltpu.make_async_copy(
            self.hbm.at[self.copy, part],
            self.local.at[self.slot, part, pl.ds(0, total)],
            self.sems.at[self.slot, part],
        )

    def start(self):
        for part in range(2):
            self.move(part).start()
            self.local[self.slot, part, self.hbm.shape[2]] = jnp.zeros((BS, BS), jnp.bfloat16)

    def wait(self, part):
        self.move(part).wait()

    def blocks(self, part):
        return self.local.at[self.slot, part]


def stage(kernel, rows_in, others, outs, scratch, slots, copies, lists, weights, flops, name):
    total = weights.shape[2]
    any_spec = pl.BlockSpec(memory_space=pl.ANY)
    smem_spec = pl.BlockSpec(memory_space=pltpu.SMEM)
    vmem_spec = pl.BlockSpec(memory_space=pltpu.VMEM)

    def body(copies_ref, lists_ref, weights_ref, *rest):
        ins, rest = rest[: len(rows_in) + len(others)], rest[len(rows_in) + len(others) :]
        results, rest = rest[: len(outs)], rest[len(outs) :]
        local, sems, rest = rest[0], rest[1], rest[2:]
        loaded = []
        for slot, which in enumerate(slots):
            copy = copies_ref[which]
            moved = Weights(weights_ref, local, sems, slot, copy)
            moved.start()
            loaded.append((Lists(lists_ref, copy, total), moved))
        kernel(loaded, ins, results, rest)

    return pl.pallas_call(
        body,
        in_specs=[smem_spec, smem_spec, any_spec]
        + [vmem_spec] * len(rows_in)
        + [any_spec] * len(others),
        out_specs=[vmem_spec if space else any_spec for space, _ in outs],
        out_shape=[shape for _, shape in outs],
        scratch_shapes=[
            pltpu.VMEM((len(slots), 2, total + 1, BS, BS), jnp.bfloat16),
            pltpu.SemaphoreType.DMA((len(slots), 2)),
        ]
        + scratch,
        name=name,
        cost_estimate=pl.CostEstimate(
            flops=flops * 8, transcendentals=0, bytes_accessed=len(slots) * weights.size
        ),
        compiler_params=pltpu.CompilerParams(vmem_limit_bytes=VMEM_LIMIT),
    )(copies, lists, weights, *rows_in, *others)


def layer_scratch(rows, width):
    return [
        pltpu.VMEM((width // BS, rows, BS), jnp.bfloat16),
        pltpu.VMEM((FF_BLOCKS, rows, BS), jnp.float32),
        pltpu.VMEM((FF_BLOCKS, rows, BS), jnp.bfloat16),
        pltpu.VMEM((width // BS, rows, BS), jnp.float32),
    ]


def slope_scratch(rows):
    return [pltpu.VMEM((FF_BLOCKS, rows, BS), jnp.float32)]


def rows_out(array):
    return (True, jax.ShapeDtypeStruct(array.shape, jnp.bfloat16))


def dense_flops(rows, weights):
    return 2 * rows * weights.shape[2] * BS * BS * 2


def forward_call(x, slots, copies, lists, weights):
    rows, width = x.shape

    def kernel(loaded, ins, results, scratch):
        source = ins[0]
        for (own_lists, moved), out in zip(loaded, results):
            forward_rows(source, out, own_lists, moved, scratch)
            source = out

    flops = dense_flops(rows, weights) * len(slots)
    return stage(
        kernel, [x], [], [rows_out(x)] * len(slots), layer_scratch(rows, width), slots, copies,
        lists, weights, flops, "forward"
    )


def turn_call(x, targets, copies, lists, weights):
    rows, width = x.shape

    def kernel(loaded, ins, results, scratch):
        x_ref, target_ref = ins
        residue, out = results
        own_lists, moved = loaded[0]
        layer, slopes = scratch[:-1], scratch[-1]
        forward_rows(x_ref, residue, own_lists, moved, layer, slopes)
        for b in range(width // BS):
            cols = slice(b * BS, (b + 1) * BS)
            difference = residue[:, cols].astype(jnp.float32) - target_ref[:, cols].astype(jnp.float32)
            residue[:, cols] = difference.astype(jnp.bfloat16)
        backward_rows(x_ref, residue, out, own_lists, moved, layer, slopes)

    return stage(
        kernel, [x, targets], [], [rows_out(x)] * 2,
        layer_scratch(rows, width) + slope_scratch(rows), [1], copies, lists, weights,
        2 * dense_flops(rows, weights), "turn"
    )


def backward_call(xs, cot, slots, copies, lists, weights):
    rows, width = cot.shape

    def kernel(loaded, ins, results, scratch):
        layer, slopes = scratch[:-1], scratch[-1]
        upstream = ins[-1]
        for (own_lists, moved), x_ref, out in zip(loaded, ins, results):
            slope_rows(x_ref, own_lists, moved, layer, slopes)
            backward_rows(x_ref, upstream, out, own_lists, moved, layer, slopes)
            upstream = out

    return stage(
        kernel, list(xs) + [cot], [], [rows_out(cot)] * len(slots),
        layer_scratch(rows, width) + slope_scratch(rows), slots, copies, lists, weights,
        2 * dense_flops(rows, weights) * len(slots), "backward"
    )


def own_layer_rows(ins, own_lists, moved, normed, split, slopes, sums, hidden, grad_pre):
    pieces = len(ins) // 2
    rows = ins[0].shape[0]
    for i in range(pieces):
        fill_normed(ins[i], normed, i * rows)
        fill_split(ins[pieces + i], split, i * rows)
    moved.wait(0)

    def finish_up(c, value):
        value, slope = both_of(value)
        hidden[c] = value.astype(jnp.bfloat16)
        slopes[c] = slope

    wide_pass(normed, moved.blocks(0), own_lists, UP_WIDE, sums, finish_up, False)
    moved.wait(1)

    def finish_down(c, value):
        grad_pre[c] = (value * slopes[c]).astype(jnp.bfloat16)

    wide_pass(split, moved.blocks(1), own_lists, DOWN_WIDE, sums, finish_down, True)


def prepare_call(pieces, copies, lists, weights):
    rows, width = pieces[0].shape
    rows = rows * len(pieces) // 2
    narrow_shape = (width // BS, BS, rows)
    wide_shape = (FF_BLOCKS, rows, BS)

    def kernel(loaded, ins, results, scratch):
        normed, split, slopes, sums, hidden, grad_pre, sems = scratch
        own_lists, moved = loaded[0]
        own_layer_rows(ins, own_lists, moved, normed, split, slopes, sums, hidden, grad_pre)
        moves = [
            pltpu.make_async_copy(source, target, sems.at[i])
            for i, (source, target) in enumerate(
                zip([hidden, grad_pre, normed, split], results)
            )
        ]
        for move in moves:
            move.start()
        for move in moves:
            move.wait()

    shapes = [wide_shape, wide_shape, (width // BS, rows, BS), (width // BS, rows, BS)]
    return stage(
        kernel, pieces, [], [(False, jax.ShapeDtypeStruct(s, jnp.bfloat16)) for s in shapes],
        [
            pltpu.VMEM((width // BS, rows, BS), jnp.bfloat16),
            pltpu.VMEM((width // BS, rows, BS), jnp.bfloat16),
            pltpu.VMEM(wide_shape, jnp.float32),
            pltpu.VMEM(wide_shape, jnp.float32),
            pltpu.VMEM(wide_shape, jnp.bfloat16),
            pltpu.VMEM(wide_shape, jnp.bfloat16),
            pltpu.SemaphoreType.DMA((4,)),
        ],
        [0], copies, lists, weights, 2 * dense_flops(rows, weights), "prepare"
    )


def grads_call(pieces, prepared, copies, lists, weights, pattern, shares):
    rows, width = pieces[0].shape
    rows = rows * len(pieces) // 2
    total = weights.shape[2]
    share_rows = BS // shares
    wide_shape = (FF_BLOCKS, rows, BS)
    pattern_flat = pattern[0].reshape(-1)

    def kernel(loaded, ins, results, scratch):
        normed, split, slopes, sums, hidden, grad_pre, turned, sems, pattern_sem, cells = scratch
        out = results[0]
        own_lists, moved = loaded[0]
        stored, pattern_ref = ins[-5:-1], ins[-1]
        load_cells = pltpu.make_async_copy(pattern_ref, cells, pattern_sem)
        load_cells.start()
        moves = [
            pltpu.make_async_copy(source, target.at[0], sems.at[i])
            for i, (source, target) in enumerate(zip(stored, [hidden, grad_pre, normed, split]))
        ]
        for move in moves:
            move.start()
        own_layer_rows(
            ins[:-5], own_lists, moved, normed.at[1], split.at[1], slopes, sums,
            hidden.at[1], grad_pre.at[1]
        )
        for move in moves:
            move.wait()
        load_cells.wait()
        for which, source in enumerate((normed, split)):
            for b in range(width // BS):
                for part in range(2):
                    turned[which, b, part] = source[part, b].T

        def one(k):
            row, col = cells[2 * k], cells[2 * k + 1]
            up = dot_plain(turned[0, row, 0], grad_pre[0, col])
            up = (up + dot_plain(turned[0, row, 1], grad_pre[1, col])).astype(jnp.bfloat16)
            row, col = cells[2 * (total + k)], cells[2 * (total + k) + 1]
            down = dot_plain(turned[1, col, 0], hidden[0, row])
            down = down + dot_plain(turned[1, col, 1], hidden[1, row])
            down = down.T.astype(jnp.bfloat16)
            for share in range(shares):
                span = slice(share * share_rows, (share + 1) * share_rows)
                out[share, 0, k] = up[span]
                out[share, 1, k] = down[span]

        each(total, one, 2)

    return stage(
        kernel, pieces, list(prepared) + [pattern_flat],
        [(True, jax.ShapeDtypeStruct((shares, 2, total, share_rows, BS), jnp.bfloat16))],
        [
            pltpu.VMEM((2, width // BS, rows, BS), jnp.bfloat16),
            pltpu.VMEM((2, width // BS, rows, BS), jnp.bfloat16),
            pltpu.VMEM(wide_shape, jnp.float32),
            pltpu.VMEM(wide_shape, jnp.float32),
            pltpu.VMEM((2,) + wide_shape, jnp.bfloat16),
            pltpu.VMEM((2,) + wide_shape, jnp.bfloat16),
            pltpu.VMEM((2, width // BS, 2, BS, rows), jnp.bfloat16),
            pltpu.SemaphoreType.DMA((4,)),
            pltpu.SemaphoreType.DMA,
            pltpu.SMEM((2 * total * 2,), jnp.int32),
        ],
        [0], copies, lists, weights, 4 * dense_flops(rows, weights), "grads"
    )[0]


def adam_update(grad_sum, master, moment, variance, token_total):
    gradient = grad_sum / token_total
    moment_next = beta_first * moment + (1.0 - beta_first) * gradient
    variance_next = beta_second * variance + (1.0 - beta_second) * gradient * gradient
    corrected = moment_next / (1.0 - beta_first**update_count)
    spread = jnp.sqrt(variance_next / (1.0 - beta_second**update_count))
    step_direction = corrected / (spread + adam_eps)
    return (step_direction, master - learn_rate * (step_direction + decay_rate * master))


def shards(tokens, targets, weights, pattern, master, moment, variance):
    section = lax.axis_index("section")
    sections = lax.axis_size("section")
    shares = lax.axis_size("dp")
    groups = sections // 2
    micro, rows_each, width = tokens.shape[1:]
    rows = micro * rows_each
    half = rows // 2
    high = section >= groups
    high_member = high.astype(jnp.int32)
    group = jnp.minimum(section, sections - 1 - section)
    copies = jnp.stack([high_member, 1 - high_member])
    own_copy = jnp.stack([jnp.zeros_like(high_member)] * 2)
    weights, pattern = weights[0], pattern[0]
    lists = block_lists(pattern)
    mirror = lambda i: sections - 1 - i

    def stream_half(array, member, h):
        stream = lax.dynamic_index_in_dim(array, member, 0, keepdims=False)
        return stream.reshape(rows, width)[h * half : (h + 1) * half]

    def lane(i, h):
        other = mirror(i + 1) if h else i + 1
        return [(i, other), (mirror(i), mirror(other))]

    def inward(x, i, h):
        return lax.ppermute(x, "section", lane(i, h))

    def outward(x, i, h):
        return lax.ppermute(x, "section", [(b, a) for a, b in lane(i, h)])

    halves = range(2)
    x_low = [[stream_half(tokens, high_member, h) for h in halves]]
    x_high, cot_low, cot_high = [[None] * groups for _ in range(3)]
    current = x_low[0]
    for i in range(groups - 1):
        current = [inward(forward_call(current[h], [0], copies, lists, weights)[0], i, h) for h in halves]
        x_low.append(current)
    both = [forward_call(current[h], [0, 1], copies, lists, weights) for h in halves]
    x_high[groups - 1] = [b[0] for b in both]
    current = [b[1] for b in both]
    for i in reversed(range(groups - 1)):
        current = [outward(current[h], i, h) for h in halves]
        x_high[i] = current
        if i > 0:
            current = [forward_call(current[h], [1], copies, lists, weights)[0] for h in halves]
    aims = [stream_half(targets, high_member, h) for h in halves]
    turned = [turn_call(current[h], aims[h], copies, lists, weights) for h in halves]
    cot_high[0] = [t[0] for t in turned]
    current = [t[1] for t in turned]
    for i in range(groups - 1):
        current = [inward(current[h], i, h) for h in halves]
        cot_high[i + 1] = current
        if i + 1 < groups - 1:
            current = [
                backward_call([x_high[i + 1][h]], current[h], [1], copies, lists, weights)[0]
                for h in halves
            ]
    last = groups - 1
    both = [
        backward_call([x_high[last][h], x_low[last][h]], current[h], [1, 0], copies, lists, weights)
        for h in halves
    ]
    cot_low[last] = [b[0] for b in both]
    current = [b[1] for b in both]
    for i in reversed(range(1, last)):
        current = [outward(current[h], i, h) for h in halves]
        cot_low[i] = current
        current = [
            backward_call([x_low[i][h]], current[h], [0], copies, lists, weights)[0] for h in halves
        ]
    from_low = [lax.ppermute(current[h], "section", [(1, 0)]) for h in halves]
    from_high = [lax.ppermute(current[h], "section", [(mirror(1), 0)]) for h in halves]

    to_low = [(mirror(i), i) for i in range(1, groups)]
    to_high = [(i, mirror(i)) for i in range(groups)]

    def at_half(records, h, start=0):
        value = records[start][h]
        for i in range(start + 1, groups):
            value = jnp.where(group == i, records[i][h], value)
        return value

    pieces = []
    first_group = (group == 0) & ~high
    for h in halves:
        x_from_high = lax.ppermute(at_half(x_low, h, 1), "section", to_low)
        x_from_low = lax.ppermute(at_half(x_high, h), "section", to_high)
        cot_from_high = lax.ppermute(at_half(cot_low, h, 1), "section", to_low)
        cot_from_low = lax.ppermute(at_half(cot_high, h), "section", to_high)
        straight, crossed = (from_high, from_low) if h else (from_low, from_high)
        x_own = jnp.where(high, at_half(x_high, h), at_half(x_low, h))
        x_other = jnp.where(
            high, x_from_low, jnp.where(group == 0, stream_half(tokens, 1, h), x_from_high)
        )
        cot_own = jnp.where(
            high, at_half(cot_high, h), jnp.where(group == 0, straight[h], at_half(cot_low, h, 1))
        )
        cot_other = jnp.where(high, cot_from_low, jnp.where(group == 0, crossed[h], cot_from_high))
        pieces.append([x_own, x_other, cot_own, cot_other])

    prepared = prepare_call(pieces[0], own_copy, lists, weights)
    grads = grads_call(pieces[1], prepared, own_copy, lists, weights, pattern, shares)
    share = lax.psum_scatter(grads, "dp", scatter_dimension=0, tiled=True)[0].astype(jnp.float32)
    token_total = 2 * rows * shares
    step_direction, master_next = adam_update(share, master[0], moment[0], variance[0], token_total)
    return (step_direction[None], master_next[None])


def solution(mesh):
    rows_split = P(None, None, "dp", None)
    by_section = P("section", None, None, "dp", None)
    return jax.shard_map(
        shards,
        mesh=mesh,
        in_specs=(
            rows_split,
            rows_split,
            P("section", None, None, None, None, None),
            P("section", None, None, None, None),
            by_section,
            by_section,
            by_section,
        ),
        out_specs=(by_section, by_section),
        check_vma=False,
    )
```

time: 430 us -> 490 us (1.14)
  Pallas kernels: 225 us -> 315 us
  waiting for transfers between devices: 147 us -> 93.2 us
  starting transfers between devices: 17.5 us -> 36.7 us
    pallas_call x5 -> x10, Pallas kernels: 225 us -> 315 us  [stage(): pl.pallas_call(body, in_specs=[smem_spec, smem_spec, any_spec] + [vmem_sp...]
    ppermute x10 -> x18, waiting for transfers between devices: 77.1 us -> 17.5 us  [the longest x2 9.07 us: shards(): from_low = [lax.ppermute(current[h], 'section', [(1, 0)]) for h in halves]]
    ppermute x10 -> x18, starting transfers between devices: 17.5 us -> 36.6 us  [the longest x4 16.3 us: inward(): return lax.ppermute(x, 'section', lane(i, h))]
    reduce_scatter x1, waiting for transfers between devices: 70.2 us -> 75.7 us  [shards(): lax.psum_scatter(grads, 'dp', scatter_dimension=0, tiled=True)[0]]
  transfers between devices with their start and end apart: 11 -> 19, of which waited for: 10 -> 3; matrix products, arithmetic and copies ran while one was open for 1% -> 2% of each run, Pallas kernels for 0% -> 52%
where the time goes in v2:
time: 490 us; the launch traced here: 485 us
  Pallas kernels  315 us (64%)
  waiting for transfers between devices  93.2 us (19%)
  starting transfers between devices  36.7 us (7%)
  other arithmetic  16.4 us (3%)
  between operations  14.6 us (3%)
  local copies, waits for them, and re-layouts  9.55 us (2%)
    pallas_call x10, Pallas kernels, stage(): pl.pallas_call(body, in_specs=[smem_spec, smem_spec, any_spec] + [vmem_sp...  315 us
    reduce_scatter x1, waiting for transfers between devices, shards(): lax.psum_scatter(grads, 'dp', scatter_dimension=0, tiled=True)[0]  75.7 us
    ppermute x4, starting transfers between devices, inward(): return lax.ppermute(x, 'section', lane(i, h))  16.3 us
  transfers between devices with their start and end apart: 19, of which 3 were waited for; matrix products, arithmetic and copies ran while one was open for 2% of the time, Pallas kernels for 52%

profile of v2, /device:TPU:0, one launch (start us, length us, event | category | flops | bytes accessed | tf_op | source)
XLA Modules:
  0.0 485.1 jit_solution(17748725162476669519)
XLA Ops:
  7.3 0.7 copy.54
  9.8 1.2 select_reduce_fusion
  11.2 0.7 reshape.315.lists_ref
  12.6 2.5 fusion.19
  15.1 15.9 %forward.6 = bf16[112,2048]{1,0:T(8,128)(2,1)} custom-call(s32[2]{0:T(128)} %pad_add_fusion.3.copies_ref, s32[6912]{0:T(1024)} %reshape.315.lists_ref, bf16[2,2,96,128,128]{4,3,2,1,0:T(8,128)(2,1)} %bitcast.129, bf16[112,2048]{1,0:T(8,128)(2,1)} %bitcast.113), custom_call_target="tpu_custom_call" | custom-call | flops 5637144576 | bytes 6291456 | tf_op jit(solution)/shard_map/forward/pallas_call | solution.py:279
  31.0 4.6 collective-permute-start.9
  35.6 16.0 %forward.4 = bf16[112,2048]{1,0:T(8,128)(2,1)} custom-call(s32[2]{0:T(128)} %pad_add_fusion.3.copies_ref, s32[6912]{0:T(1024)} %reshape.315.lists_ref, bf16[2,2,96,128,128]{4,3,2,1,0:T(8,128)(2,1)} %bitcast.130, bf16[112,2048]{1,0:T(8,128)(2,1)} %bitcast.112), custom_call_target="tpu_custom_call" | custom-call | flops 5637144576 | bytes 6291456 | tf_op jit(solution)/shard_map/forward/pallas_call | solution.py:279
  51.5 1.3 collective-permute-start
  53.0 0.7 reshape_squeeze.3.rest_8_
  53.8 2.2 constant_dynamic-slice_fusion.1
  55.9 0.8 copy-done.6
  56.7 29.0 %forward.7 = (bf16[112,2048]{1,0:T(8,128)(2,1)}, bf16[112,2048]{1,0:T(8,128)(2,1)}) custom-call(s32[2]{0:T(128)} %pad_add_fusion.3.copies_ref, s32[6912]{0:T(1024)} %reshape.315.lists_ref, bf16[2,2,96,128,128]{4,3,2,1,0:T(8,128)(2,1)} %bitcast.131, bf16[112,2048]{1,0:T(8,128)(2,1)} %copy-done.6), custom_call_target="tpu_custom_call" | custom-call | flops 11274289152 | bytes 12582912 | tf_op jit(solution)/shard_map/forward/pallas_call | solution.py:279
  85.8 1.4 collective-permute-start.10
  87.2 0.8 copy-done.4
  88.0 29.0 %forward.5 = (bf16[112,2048]{1,0:T(8,128)(2,1)}, bf16[112,2048]{1,0:T(8,128)(2,1)}) custom-call(s32[2]{0:T(128)} %pad_add_fusion.3.copies_ref, s32[6912]{0:T(1024)} %reshape.315.lists_ref, bf16[2,2,96,128,128]{4,3,2,1,0:T(8,128)(2,1)} %bitcast.132, bf16[112,2048]{1,0:T(8,128)(2,1)} %copy-done.4), custom_call_target="tpu_custom_call" | custom-call | flops 11274289152 | bytes 12582912 | tf_op jit(solution)/shard_map/forward/pallas_call | solution.py:279
  117.1 1.3 collective-permute-start.1
  118.4 1.4 collective-permute-start.3
  119.8 1.4 collective-permute-start.12
  121.2 0.9 select_select_fusion.2
  122.2 4.2 collective-permute-start.11
  126.4 30.4 %turn.3 = (bf16[112,2048]{1,0:T(8,128)(2,1)}, bf16[112,2048]{1,0:T(8,128)(2,1)}) custom-call(s32[2]{0:T(128)} %pad_add_fusion.3.copies_ref, s32[6912]{0:T(1024)} %reshape.315.lists_ref, bf16[2,2,96,128,128]{4,3,2,1,0:T(8,128)(2,1)} %bitcast.133, bf16[112,2048]{1,0:T(8,128)(2,1)} %copy-done.10, bf16[112,2048]{1,0:T(8,128)(2,1)} %bitcast.115), custom_call_target="tpu_custom_call" | custom-call | flops 11274289152 | bytes 6291456 | tf_op jit(solution)/shard_map/turn/pallas_call | solution.py:279
  156.7 9.1 %collective-permute-start.13 = (bf16[112,2048]{1,0:T(8,128)(2,1)}, bf16[112,2048]{1,0:T(8,128)(2,1)}, u32[]{:S(2)}, u32[]{:S(2)}) collective-permute-start(bf16[112,2048]{1,0:T(8,128)(2,1)} %get-tuple-element.26), channel_id=1, source_target_pairs={{0,8},{24,16},{1,9},{25,17},{2,10},{26,18},{3,11},{27,19},{4,12},{... | collective-permute-start | bytes 1376264 | tf_op jit(solution)/shard_map/ppermute | solution.py:538
  165.8 1.9 select_select_fusion.5
  167.7 1.3 collective-permute-start.2
  169.1 30.2 %turn.2 = (bf16[112,2048]{1,0:T(8,128)(2,1)}, bf16[112,2048]{1,0:T(8,128)(2,1)}) custom-call(s32[2]{0:T(128)} %pad_add_fusion.3.copies_ref, s32[6912]{0:T(1024)} %reshape.315.lists_ref, bf16[2,2,96,128,128]{4,3,2,1,0:T(8,128)(2,1)} %bitcast.134, bf16[112,2048]{1,0:T(8,128)(2,1)} %collective-permute-done.1.rest_0_, bf16[112,2048]{1,0:T(8,128)(2,1)} %bitcast.114), custom_call_target="tpu_custom_call" | custom-call | flops 11274289152 | bytes 6291456 | tf_op jit(solution)/shard_map/turn/pallas_call | solution.py:279
  199.3 1.3 collective-permute-start.4
  200.6 46.7 %backward.3 = (bf16[112,2048]{1,0:T(8,128)(2,1)}, bf16[112,2048]{1,0:T(8,128)(2,1)}) custom-call(s32[2]{0:T(128)} %pad_add_fusion.3.copies_ref, s32[6912]{0:T(1024)} %reshape.315.lists_ref, bf16[2,2,96,128,128]{4,3,2,1,0:T(8,128)(2,1)} %bitcast.135, bf16[112,2048]{1,0:T(8,128)(2,1)} %get-tuple-element.24.rest_0_, bf16[112,2048]{1,0:T(8,128)(2,1)} %copy-done.6, ...), custom_call_target="tpu_custom_call" | custom-call | flops 22548578304 | bytes 12582912 | tf_op jit(solution)/shard_map/backward/pallas_call | solution.py:279
  247.4 1.3 collective-permute-start.16
  248.7 46.9 %backward.2 = (bf16[112,2048]{1,0:T(8,128)(2,1)}, bf16[112,2048]{1,0:T(8,128)(2,1)}) custom-call(s32[2]{0:T(128)} %pad_add_fusion.3.copies_ref, s32[6912]{0:T(1024)} %reshape.315.lists_ref, bf16[2,2,96,128,128]{4,3,2,1,0:T(8,128)(2,1)} %bitcast.136, bf16[112,2048]{1,0:T(8,128)(2,1)} %get-tuple-element.18.rest_0_, bf16[112,2048]{1,0:T(8,128)(2,1)} %copy-done.4, ...), custom_call_target="tpu_custom_call" | custom-call | flops 22548578304 | bytes 12582912 | tf_op jit(solution)/shard_map/backward/pallas_call | solution.py:279
  295.6 1.4 collective-permute-start.14
  297.1 1.3 collective-permute-start.7
  298.4 0.9 fusion.8.rest_1_
  299.3 1.3 collective-permute-start.5
  300.6 0.7 collective-permute-start.17
  301.3 0.9 fusion.9.rest_1_
  302.2 9.1 %collective-permute-done.14 = bf16[112,2048]{1,0:T(8,128)(2,1)S(1)} collective-permute-done((bf16[112,2048]{1,0:T(8,128)(2,1)}, bf16[112,2048]{1,0:T(8,128)(2,1)S(1)}, u32[]{:S(2)}, u32[]{:S(2)}) %collective-permute-start.14) | collective-permute-done | bytes 458784 | tf_op jit(solution)/shard_map/ppermute | solution.py:583
  311.3 0.7 collective-permute-start.8
  312.0 0.9 select_select_fusion.1
  312.8 1.3 collective-permute-start.15
  314.2 1.1 select_select_fusion.4
  315.3 1.3 collective-permute-start.6
  316.6 8.4 %collective-permute-done.15 = bf16[112,2048]{1,0:T(8,128)(2,1)S(1)} collective-permute-done((bf16[112,2048]{1,0:T(8,128)(2,1)S(1)}, bf16[112,2048]{1,0:T(8,128)(2,1)S(1)}, u32[]{:S(2)}, u32[]{:S(2)}) %collective-permute-start.15) | collective-permute-done | bytes 458784 | tf_op jit(solution)/shard_map/ppermute | solution.py:601
  325.0 0.9 select_select_fusion.rest_3_
  326.4 25.5 %prepare.1 = (bf16[64,224,128]{2,1,0:T(8,128)(2,1)}, bf16[64,224,128]{2,1,0:T(8,128)(2,1)}, bf16[16,224,128]{2,1,0:T(8,128)(2,1)}, bf16[16,224,128]{2,1,0:T(8,128)(2,1)}) custom-call(s32[2]{0:T(128)} %broadcast_11_copies_ref.2.copies_ref, s32[6912]{0:T(1024)} %reshape.315.lists_ref, bf16[2,2,96,128,128]{4,3,2,1,0:T(8,128)(2,1)} %bitcast.137, ...), custom_call_target="tpu_custom_call" | custom-call | flops 22548578304 | bytes 6291456 | tf_op jit(solution)/shard_map/prepare/pallas_call | solution.py:279
  352.0 0.8 select_select_fusion.3.rest_3_
  352.8 45.1 %grads.1 = bf16[8,2,96,16,128]{4,3,2,1,0:T(8,128)(2,1)} custom-call(s32[2]{0:T(128)} %broadcast_11_copies_ref.2.copies_ref, s32[6912]{0:T(1024)} %reshape.315.lists_ref, bf16[2,2,96,128,128]{4,3,2,1,0:T(8,128)(2,1)} %bitcast.138, bf16[112,2048]{1,0:T(8,128)(2,1)} %get-tuple-element.42.rest_0_, bf16[112,2048]{1,0:T(8,128)(2,1)} %fusion.9.rest_1_, ...), custom_call_target="tpu_custom_call" | custom-call | flops 45097156608 | bytes 6291456 | tf_op jit(solution)/shard_map/grads/pallas_call | solution.py:279
  398.0 75.7 %reduce-scatter.2.cloned.1.call-done = bf16[1,2,96,16,128]{4,3,2,1,0:T(8,128)(2,1)} async-done(((bf16[8,2,96,16,128]{4,3,2,1,0:T(8,128)(2,1)}), bf16[1,2,96,16,128]{4,3,2,1,0:T(8,128)(2,1)}) %reduce-scatter.2.cloned.1.call-update) | async-done | bytes 786448 | tf_op jit(solution)/shard_map/reduce_scatter | solution.py:615
  473.7 4.6 multiply_subtract_fusion
  (92 shorter events, 3.5 us)
Async XLA Ops:
  7.2 466.5 %reduce-scatter.2.cloned.1.call-start = ((), (), s32[]{:S(2)}) async-start(), calls=%async_computation.1 | async-start | bytes 7077888 | tf_op jit(solution)/shard_map/reduce_scatter | solution.py:615
  31.0 25.0 %collective-permute-start.9 = (bf16[112,2048]{1,0:T(8,128)(2,1)}, bf16[112,2048]{1,0:T(8,128)(2,1)S(1)}, u32[]{:S(2)}, u32[]{:S(2)}) collective-permute-start(bf16[112,2048]{1,0:T(8,128)(2,1)} %forward.6), channel_id=1, source_target_pairs={{0,8},{24,16},{1,9},{25,17},{2,10},{26,18},{3,11},{27,19},{4,12},{... | collective-permute-start | bytes 1376264 | tf_op jit(solution)/shard_map/ppermute | solution.py:538
  35.5 17.3 %slice-start = ((s32[1,2,2,96,2]{3,4,2,1,0:T(2,128)}), s32[1,1,2,96,2]{3,4,2,1,0:T(2,128)S(1)}, s32[]{:S(2)}) async-start(s32[1,2,2,96,2]{3,4,2,1,0:T(2,128)} %param.10), calls=%async_computation.2 | async-start | bytes 4096 | tf_op jit(solution)/shard_map/slice | solution.py:441
  51.5 35.7 %collective-permute-start = (bf16[112,2048]{1,0:T(8,128)(2,1)}, bf16[112,2048]{1,0:T(8,128)(2,1)S(1)}, u32[]{:S(2)}, u32[]{:S(2)}) collective-permute-start(bf16[112,2048]{1,0:T(8,128)(2,1)} %forward.4), channel_id=1, source_target_pairs={{0,16},{24,8},{1,17},{25,9},{2,18},{26,10},{3,19},{27,11},{4,20},{... | collective-permute-start | bytes 1376264 | tf_op jit(solution)/shard_map/ppermute | solution.py:538
  55.9 0.8 copy-start.6
  85.8 34.0 %copy-start.7 = (bf16[112,2048]{1,0:T(8,128)(2,1)S(1)}, bf16[112,2048]{1,0:T(8,128)(2,1)}, u32[]{:S(2)}) copy-start(bf16[112,2048]{1,0:T(8,128)(2,1)} %copy-done.6) | copy-start | bytes 1376260
  85.8 35.5 %copy-start.1 = (bf16[1,2,56,2048]{3,2,1,0:T(8,128)(2,1)S(1)}, bf16[1,2,56,2048]{3,2,1,0:T(8,128)(2,1)}, u32[]{:S(2)}) copy-start(bf16[1,2,56,2048]{3,2,1,0:T(8,128)(2,1)} %get-tuple-element.56) | copy-start | bytes 1376260
  85.8 35.5 %copy-start.9 = (bf16[112,2048]{1,0:T(8,128)(2,1)S(1)}, bf16[112,2048]{1,0:T(8,128)(2,1)}, u32[]{:S(2)}) copy-start(bf16[112,2048]{1,0:T(8,128)(2,1)} %get-tuple-element.24.rest_0_) | copy-start | bytes 1376260
  85.8 35.4 %collective-permute-start.10 = (bf16[112,2048]{1,0:T(8,128)(2,1)}, bf16[112,2048]{1,0:T(8,128)(2,1)S(1)}, u32[]{:S(2)}, u32[]{:S(2)}) collective-permute-start(bf16[112,2048]{1,0:T(8,128)(2,1)} %get-tuple-element.25), channel_id=1, source_target_pairs={{8,0},{16,24},{9,1},{17,25},{10,2},{18,26},{11,3},{19,27},{12,4},{... | collective-permute-start | bytes 1376264 | tf_op jit(solution)/shard_map/ppermute | solution.py:541
  87.2 0.8 copy-start.4
  117.1 48.8 %collective-permute-start.1 = (bf16[112,2048]{1,0:T(8,128)(2,1)}, bf16[112,2048]{1,0:T(8,128)(2,1)}, u32[]{:S(2)}, u32[]{:S(2)}) collective-permute-start(bf16[112,2048]{1,0:T(8,128)(2,1)} %get-tuple-element.19), channel_id=1, source_target_pairs={{16,0},{8,24},{17,1},{9,25},{18,2},{10,26},{19,3},{11,27},{20,4},{... | collective-permute-start | bytes 1376264 | tf_op jit(solution)/shard_map/ppermute | solution.py:541
  118.4 180.9 %collective-permute-start.3 = (bf16[112,2048]{1,0:T(8,128)(2,1)}, bf16[112,2048]{1,0:T(8,128)(2,1)}, u32[]{:S(2)}, u32[]{:S(2)}) collective-permute-start(bf16[112,2048]{1,0:T(8,128)(2,1)} %copy-done.4), channel_id=1, source_target_pairs={{16,8},{17,9},{18,10},{19,11},{20,12},{21,13},{22,14},{23,15}} | collective-permute-start | bytes 1376264 | tf_op jit(solution)/shard_map/ppermute | solution.py:598
  119.8 175.8 %collective-permute-start.12 = (bf16[112,2048]{1,0:T(8,128)(2,1)S(1)}, bf16[112,2048]{1,0:T(8,128)(2,1)}, u32[]{:S(2)}, u32[]{:S(2)}) collective-permute-start(bf16[112,2048]{1,0:T(8,128)(2,1)S(1)} %copy-done.7), channel_id=1, source_target_pairs={{16,8},{17,9},{18,10},{19,11},{20,12},{21,13},{22,14},{23,15}} | collective-permute-start | bytes 1376264 | tf_op jit(solution)/shard_map/ppermute | solution.py:598
  121.2 5.1 %copy-start.10 = (bf16[112,2048]{1,0:T(8,128)(2,1)}, bf16[112,2048]{1,0:T(8,128)(2,1)S(1)}, u32[]{:S(2)}) copy-start(bf16[112,2048]{1,0:T(8,128)(2,1)S(1)} %collective-permute-done.10.rest_0_) | copy-start | bytes 1376260
  122.2 174.9 %collective-permute-start.11 = (bf16[112,2048]{1,0:T(8,128)(2,1)S(1)}, bf16[112,2048]{1,0:T(8,128)(2,1)}, u32[]{:S(2)}, u32[]{:S(2)}) collective-permute-start(bf16[112,2048]{1,0:T(8,128)(2,1)S(1)} %get-tuple-element.39), channel_id=1, source_target_pairs={{0,24},{8,16},{1,25},{9,17},{2,26},{10,18},{3,27},{11,19},{4,28},{... | collective-permute-start | bytes 1376264 | tf_op jit(solution)/shard_map/ppermute | solution.py:599
  126.4 39.5 %copy-start = (bf16[1,2,56,2048]{3,2,1,0:T(8,128)(2,1)S(1)}, bf16[1,2,56,2048]{3,2,1,0:T(8,128)(2,1)}, u32[]{:S(2)}) copy-start(bf16[1,2,56,2048]{3,2,1,0:T(8,128)(2,1)} %get-tuple-element.55) | copy-start | bytes 1376260
  126.4 39.5 %copy-start.5 = (bf16[112,2048]{1,0:T(8,128)(2,1)S(1)}, bf16[112,2048]{1,0:T(8,128)(2,1)}, u32[]{:S(2)}) copy-start(bf16[112,2048]{1,0:T(8,128)(2,1)} %copy-done.4) | copy-start | bytes 1376260
  126.4 39.5 %copy-start.8 = (bf16[112,2048]{1,0:T(8,128)(2,1)S(1)}, bf16[112,2048]{1,0:T(8,128)(2,1)}, u32[]{:S(2)}) copy-start(bf16[112,2048]{1,0:T(8,128)(2,1)} %get-tuple-element.18.rest_0_) | copy-start | bytes 1376260
  156.7 42.6 %collective-permute-start.13 = (bf16[112,2048]{1,0:T(8,128)(2,1)}, bf16[112,2048]{1,0:T(8,128)(2,1)}, u32[]{:S(2)}, u32[]{:S(2)}) collective-permute-start(bf16[112,2048]{1,0:T(8,128)(2,1)} %get-tuple-element.26), channel_id=1, source_target_pairs={{0,8},{24,16},{1,9},{25,17},{2,10},{26,18},{3,11},{27,19},{4,12},{... | collective-permute-start | bytes 1376264 | tf_op jit(solution)/shard_map/ppermute | solution.py:538
  167.7 132.8 %collective-permute-start.2 = (bf16[112,2048]{1,0:T(8,128)(2,1)S(1)}, bf16[112,2048]{1,0:T(8,128)(2,1)S(1)}, u32[]{:S(2)}, u32[]{:S(2)}) collective-permute-start(bf16[112,2048]{1,0:T(8,128)(2,1)S(1)} %get-tuple-element.43), channel_id=1, source_target_pairs={{0,24},{8,16},{1,25},{9,17},{2,26},{10,18},{3,27},{11,19},{4,28},{... | collective-permute-start | bytes 1376264 | tf_op jit(solution)/shard_map/ppermute | solution.py:599
  199.3 48.1 %collective-permute-start.4 = (bf16[112,2048]{1,0:T(8,128)(2,1)}, bf16[112,2048]{1,0:T(8,128)(2,1)S(1)}, u32[]{:S(2)}, u32[]{:S(2)}) collective-permute-start(bf16[112,2048]{1,0:T(8,128)(2,1)} %get-tuple-element.20), channel_id=1, source_target_pairs={{0,16},{24,8},{1,17},{25,9},{2,18},{26,10},{3,19},{27,11},{4,20},{... | collective-permute-start | bytes 1376264 | tf_op jit(solution)/shard_map/ppermute | solution.py:538
  247.4 1.3 copy-start.15
  247.4 67.9 %collective-permute-start.16 = (bf16[112,2048]{1,0:T(8,128)(2,1)}, bf16[112,2048]{1,0:T(8,128)(2,1)S(1)}, u32[]{:S(2)}, u32[]{:S(2)}) collective-permute-start(bf16[112,2048]{1,0:T(8,128)(2,1)} %get-tuple-element.28), channel_id=1, source_target_pairs={{16,0},{17,1},{18,2},{19,3},{20,4},{21,5},{22,6},{23,7}} | collective-permute-start | bytes 1376264 | tf_op jit(solution)/shard_map/ppermute | solution.py:584
  295.6 3.7 copy-start.17
  295.6 5.0 %copy-start.14 = (bf16[112,2048]{1,0:T(8,128)(2,1)S(1)}, bf16[112,2048]{1,0:T(8,128)(2,1)}, u32[]{:S(2)}) copy-start(bf16[112,2048]{1,0:T(8,128)(2,1)} %get-tuple-element.29) | copy-start | bytes 1376260
  295.6 15.6 %collective-permute-start.14 = (bf16[112,2048]{1,0:T(8,128)(2,1)}, bf16[112,2048]{1,0:T(8,128)(2,1)S(1)}, u32[]{:S(2)}, u32[]{:S(2)}) collective-permute-start(bf16[112,2048]{1,0:T(8,128)(2,1)} %get-tuple-element.28), channel_id=1, source_target_pairs={{8,0},{9,1},{10,2},{11,3},{12,4},{13,5},{14,6},{15,7}} | collective-permute-start | bytes 1376264 | tf_op jit(solution)/shard_map/ppermute | solution.py:583
  297.1 54.9 %collective-permute-start.7 = (bf16[112,2048]{1,0:T(8,128)(2,1)}, bf16[112,2048]{1,0:T(8,128)(2,1)S(1)}, u32[]{:S(2)}, u32[]{:S(2)}) collective-permute-start(bf16[112,2048]{1,0:T(8,128)(2,1)} %get-tuple-element.22), channel_id=1, source_target_pairs={{8,0},{9,1},{10,2},{11,3},{12,4},{13,5},{14,6},{15,7}} | collective-permute-start | bytes 1376264 | tf_op jit(solution)/shard_map/ppermute | solution.py:583
  298.4 12.9 %copy-start.11 = (bf16[112,2048]{1,0:T(8,128)(2,1)S(1)}, bf16[112,2048]{1,0:T(8,128)(2,1)}, u32[]{:S(2)}) copy-start(bf16[112,2048]{1,0:T(8,128)(2,1)} %get-tuple-element.23) | copy-start | bytes 1376260
  298.4 13.6 %copy-start.12 = (bf16[112,2048]{1,0:T(8,128)(2,1)S(1)}, bf16[112,2048]{1,0:T(8,128)(2,1)}, u32[]{:S(2)}) copy-start(bf16[112,2048]{1,0:T(8,128)(2,1)} %get-tuple-element.27) | copy-start | bytes 1376260
  299.3 13.6 %collective-permute-start.5 = (bf16[112,2048]{1,0:T(8,128)(2,1)S(1)}, bf16[112,2048]{1,0:T(8,128)(2,1)S(1)}, u32[]{:S(2)}, u32[]{:S(2)}) collective-permute-start(bf16[112,2048]{1,0:T(8,128)(2,1)S(1)} %copy-done.17), channel_id=1, source_target_pairs={{16,0},{17,1},{18,2},{19,3},{20,4},{21,5},{22,6},{23,7}} | collective-permute-start | bytes 1376264 | tf_op jit(solution)/shard_map/ppermute | solution.py:584
  300.6 16.0 %collective-permute-start.17 = (bf16[112,2048]{1,0:T(8,128)(2,1)S(1)}, bf16[112,2048]{1,0:T(8,128)(2,1)S(1)}, u32[]{:S(2)}, u32[]{:S(2)}) collective-permute-start(bf16[112,2048]{1,0:T(8,128)(2,1)S(1)} %copy-done.14), channel_id=1, source_target_pairs={{16,8},{17,9},{18,10},{19,11},{20,12},{21,13},{22,14},{23,15}} | collective-permute-start | bytes 1376264 | tf_op jit(solution)/shard_map/ppermute | solution.py:600
  302.2 12.0 %copy-start.13 = (bf16[112,2048]{1,0:T(8,128)(2,1)S(1)}, bf16[112,2048]{1,0:T(8,128)(2,1)}, u32[]{:S(2)}) copy-start(bf16[112,2048]{1,0:T(8,128)(2,1)} %get-tuple-element.21) | copy-start | bytes 1376260
  302.2 12.0 %copy-start.16 = (bf16[112,2048]{1,0:T(8,128)(2,1)S(1)}, bf16[112,2048]{1,0:T(8,128)(2,1)}, u32[]{:S(2)}) copy-start(bf16[112,2048]{1,0:T(8,128)(2,1)} %copy-done.15) | copy-start | bytes 1376260
  311.3 40.7 %collective-permute-start.8 = (bf16[112,2048]{1,0:T(8,128)(2,1)S(1)}, bf16[112,2048]{1,0:T(8,128)(2,1)S(1)}, u32[]{:S(2)}, u32[]{:S(2)}) collective-permute-start(bf16[112,2048]{1,0:T(8,128)(2,1)S(1)} %copy-done.11), channel_id=1, source_target_pairs={{16,8},{17,9},{18,10},{19,11},{20,12},{21,13},{22,14},{23,15}} | collective-permute-start | bytes 1376264 | tf_op jit(solution)/shard_map/ppermute | solution.py:600
  312.8 12.2 %collective-permute-start.15 = (bf16[112,2048]{1,0:T(8,128)(2,1)S(1)}, bf16[112,2048]{1,0:T(8,128)(2,1)S(1)}, u32[]{:S(2)}, u32[]{:S(2)}) collective-permute-start(bf16[112,2048]{1,0:T(8,128)(2,1)S(1)} %get-tuple-element.37), channel_id=1, source_target_pairs={{0,24},{8,16},{1,25},{9,17},{2,26},{10,18},{3,27},{11,19},{4,28},{... | collective-permute-start | bytes 1376264 | tf_op jit(solution)/shard_map/ppermute | solution.py:601
  315.3 36.7 %collective-permute-start.6 = (bf16[112,2048]{1,0:T(8,128)(2,1)}, bf16[112,2048]{1,0:T(8,128)(2,1)S(1)}, u32[]{:S(2)}, u32[]{:S(2)}) collective-permute-start(bf16[112,2048]{1,0:T(8,128)(2,1)} %get-tuple-element.41), channel_id=1, source_target_pairs={{0,24},{8,16},{1,25},{9,17},{2,26},{10,18},{3,27},{11,19},{4,28},{... | collective-permute-start | bytes 1376264 | tf_op jit(solution)/shard_map/ppermute | solution.py:601
  398.0 75.7 %copy-start.2 = (f32[1,2,96,16,128]{4,3,2,1,0:T(8,128)S(1)}, f32[1,2,96,16,128]{4,3,2,1,0:T(8,128)}, u32[]{:S(2)}) copy-start(f32[1,2,96,16,128]{4,3,2,1,0:T(8,128)} %param.11) | copy-start | bytes 4718596
  398.0 75.7 %copy-start.3 = (f32[1,2,96,16,128]{4,3,2,1,0:T(8,128)S(1)}, f32[1,2,96,16,128]{4,3,2,1,0:T(8,128)}, u32[]{:S(2)}) copy-start(f32[1,2,96,16,128]{4,3,2,1,0:T(8,128)} %param.13) | copy-start | bytes 4718596
Sparse Core Ops, SparseCore 0:
  398.1 75.5 reduce-scatter.1
